TPU v7x, 128 devices: a whole 4x4x4 slice. The times are simulated.
128 devices in a mesh: tiles: 16 (over y, z), lag: 8 (over x, core).
Axes of the slice: x: 4, y: 4, z: 4, core: 2. Of those that a mesh axis runs over, the one named last changes fastest.
Arguments:
- spectra: bfloat16 [32, 2, 2, 128, 8192], P('tiles', None, None, None, 'lag'), may hold values from -6 to 6
- requests: int32 [16, 6], replicated, may hold values from 0 to 31, as said below
- pairs: int32 [16, 3, 2], P('tiles'), may hold values from 0 to 5, as said below
- counts: int32 [16], P('tiles'), may hold values from 2 to 3, as said below
Outputs:
- stacked_lags: float32 [48, 64, 128, 128], P('tiles', 'lag')
Inputs may be any that keep to these rules, and one draw needn't show every extreme that they name: Block b is held by index b // 2 of tiles; each row of requests names 6 blocks held by 6 different indices. Each row's 3 entries are pairs (i, j) of request slots with i < j that together use every request slot once. The first counts[d] slots of row d are live, the others give zeros; some index has 3.
All inputs are finite; a program needn't handle non-finite values.
Results may differ from a plain program's by a relative error of at most 0.012.
Values may be sent and summed in bfloat16 or wider, within the bound.
A program may use at most 128 MiB of HBM per device.

v0:
```python
import math

import jax
import jax.numpy as jnp
from jax import lax
from jax.sharding import PartitionSpec as P

F = 8192
W = 2
LAGS = 64
FBLK = 128


def phase_table(freq_first, width):
    frequencies = freq_first + jnp.arange(width, dtype=jnp.int32)
    shifts = (jnp.arange(LAGS, dtype=jnp.int32) - LAGS // 2) % F
    phase_index = frequencies[:, None] * shifts[None, :] % F
    angles = phase_index.astype(jnp.float32) * (2.0 * math.pi / F)
    return jnp.concatenate([jnp.cos(angles), -jnp.sin(angles)], axis=0).astype(jnp.bfloat16)


def cross_block(left_part, right_part):
    left_wide = left_part.astype(jnp.float32)
    right_wide = right_part.astype(jnp.float32)
    real_part = jnp.sum(
        left_wide[:, 0, :, None, :] * right_wide[:, 0, None, :, :]
        + left_wide[:, 1, :, None, :] * right_wide[:, 1, None, :, :],
        axis=0,
    )
    imag_part = jnp.sum(
        left_wide[:, 1, :, None, :] * right_wide[:, 0, None, :, :]
        - left_wide[:, 0, :, None, :] * right_wide[:, 1, None, :, :],
        axis=0,
    )
    channels = left_part.shape[2]
    return (
        jnp.concatenate([real_part, imag_part], axis=-1)
        .reshape(channels * channels, -1)
        .astype(jnp.bfloat16)
    )


def band_sum(left_block, right_block, band_first):
    channels = left_block.shape[2]
    block_count = left_block.shape[-1] // FBLK

    def block_step(running, block_index):
        offset = block_index * FBLK
        left_part = lax.dynamic_slice_in_dim(left_block, offset, FBLK, 3)
        right_part = lax.dynamic_slice_in_dim(right_block, offset, FBLK, 3)
        stacked = cross_block(left_part, right_part)
        phases = phase_table(band_first + offset, FBLK)
        return (
            running
            + lax.dot_general(
                phases, stacked, (((0,), (1,)), ((), ())), preferred_element_type=jnp.float32
            ),
            None,
        )

    running = jnp.zeros((LAGS, channels * channels), jnp.float32)
    running, unused = lax.scan(block_step, running, jnp.arange(block_count, dtype=jnp.int32))
    return running


def per_device(spectra, requests, pairs, counts):
    channels = spectra.shape[3]
    own_index = lax.axis_index("tiles")
    wanted = lax.dynamic_index_in_dim(requests, own_index, 0, keepdims=False)
    empty = jnp.zeros((wanted.shape[0],) + spectra.shape[1:], jnp.bfloat16)
    shards = lax.all_gather(spectra, "tiles", axis=0, tiled=True)
    inside = (wanted >= 0) & (wanted < shards.shape[0])
    taken = jnp.take(shards, jnp.clip(wanted, 0, shards.shape[0] - 1), axis=0)
    needed = jnp.where(inside[:, None, None, None, None], taken, empty)
    band_first = lax.axis_index("lag") * spectra.shape[-1]
    norm_factor = 1.0 / math.sqrt(2.0 * W * F)
    live_count = counts[0]
    tile_pairs = pairs[0]
    slot_total = tile_pairs.shape[0]
    terms = []
    for slot_index in range(slot_total):
        left_block = jnp.take(needed, tile_pairs[slot_index, 0], axis=0)
        right_block = jnp.take(needed, tile_pairs[slot_index, 1], axis=0)
        result = band_sum(left_block, right_block, band_first) * norm_factor
        terms.append(jnp.where(slot_index < live_count, result, jnp.zeros_like(result)))
    partial_terms = jnp.stack(terms).reshape(slot_total, LAGS, channels, channels)
    return lax.psum_scatter(
        partial_terms.astype(jnp.bfloat16), "lag", scatter_dimension=1, tiled=True
    ).astype(jnp.float32)


def solution(mesh):
    placed = (P("tiles", None, None, None, "lag"), P(), P("tiles", None, None), P("tiles"))
    return jax.shard_map(
        per_device,
        mesh=mesh,
        in_specs=placed,
        out_specs=P("tiles", "lag", None, None),
        check_vma=False,
    )
```

profile of v0, /device:TPU:1, one launch (start us, length us, event | category | flops | bytes accessed | tf_op | source)
XLA Modules:
  0.0 1019.3 jit_solution(7977212312652234884)
XLA Ops:
  22.7 187.3 %all-gather.2.cloned.1.call-done = bf16[32,2,2,128,1024]{4,3,2,1,0:T(8,128)(2,1)} async-done(((bf16[2,2,2,128,1024]{4,3,2,1,0:T(8,128)(2,1)}), bf16[32,2,2,128,1024]{4,3,2,1,0:T(8,128)(2,1)}) %all-gather.2.cloned.1.call-update) | async-done | bytes 33554448 | tf_op jit(solution)/shard_map/all_gather | solution.py:71
  222.7 236.0 %while.40 = (s32[]{:T(128)}, f32[64,16384]{1,0:T(8,128)}, s32[8]{0:T(128)S(1)}, s32[]{:T(128)}, bf16[2,2,128,1024]{3,2,1,0:T(8,128)(2,1)S(1)}, /*index=5*/bf16[2...) while((s32[]{:T(128)}, f32[64,16384]{1,0:T(8,128)}, ...), condition=%wide.region_3.5_spmd.clone, body=%wide.region_0.0_spmd.clone.sunk | while | flops 585442176 | bytes 44893884 | solution.py:62
  224.2 11.7 %add_reduce_fusion.6 = (bf16[128,128,128]{2,1,0:T(8,128)(2,1)S(1)}, bf16[128,128,128]{2,1,0:T(8,128)(2,1)}) fusion(f32[2,128,128]{2,1,0:T(8,128)S(1)} %get-tuple-element.564, f32[2,128,128]{2,1,0:T(8,128)S(1)} %get-tuple-element.566, f32[2,128,128]{2,1,0:T(8,128)S(1)} %get-tuple-element.567, f32[2,128,128]{2,1,0:T(8,128)S(1)} %get-tuple-element.568), kind=kLoop, calls=%fused_computation.3.clone.1 | loop fusion | flops 29360128 | bytes 8912896 | tf_op jit(solution)/shard_map/while/body/eval_jaxpr/reduce_sum | solution.py:25
  252.7 11.7 %add_reduce_fusion.6 = (bf16[128,128,128]{2,1,0:T(8,128)(2,1)S(1)}, bf16[128,128,128]{2,1,0:T(8,128)(2,1)}) fusion(f32[2,128,128]{2,1,0:T(8,128)S(1)} %get-tuple-element.564, f32[2,128,128]{2,1,0:T(8,128)S(1)} %get-tuple-element.566, f32[2,128,128]{2,1,0:T(8,128)S(1)} %get-tuple-element.567, f32[2,128,128]{2,1,0:T(8,128)S(1)} %get-tuple-element.568), kind=kLoop, calls=%fused_computation.3.clone.1 | loop fusion | flops 29360128 | bytes 8912896 | tf_op jit(solution)/shard_map/while/body/eval_jaxpr/reduce_sum | solution.py:25
  282.4 11.7 %add_reduce_fusion.6 = (bf16[128,128,128]{2,1,0:T(8,128)(2,1)S(1)}, bf16[128,128,128]{2,1,0:T(8,128)(2,1)}) fusion(f32[2,128,128]{2,1,0:T(8,128)S(1)} %get-tuple-element.564, f32[2,128,128]{2,1,0:T(8,128)S(1)} %get-tuple-element.566, f32[2,128,128]{2,1,0:T(8,128)S(1)} %get-tuple-element.567, f32[2,128,128]{2,1,0:T(8,128)S(1)} %get-tuple-element.568), kind=kLoop, calls=%fused_computation.3.clone.1 | loop fusion | flops 29360128 | bytes 8912896 | tf_op jit(solution)/shard_map/while/body/eval_jaxpr/reduce_sum | solution.py:25
  312.0 11.7 %add_reduce_fusion.6 = (bf16[128,128,128]{2,1,0:T(8,128)(2,1)S(1)}, bf16[128,128,128]{2,1,0:T(8,128)(2,1)}) fusion(f32[2,128,128]{2,1,0:T(8,128)S(1)} %get-tuple-element.564, f32[2,128,128]{2,1,0:T(8,128)S(1)} %get-tuple-element.566, f32[2,128,128]{2,1,0:T(8,128)S(1)} %get-tuple-element.567, f32[2,128,128]{2,1,0:T(8,128)S(1)} %get-tuple-element.568), kind=kLoop, calls=%fused_computation.3.clone.1 | loop fusion | flops 29360128 | bytes 8912896 | tf_op jit(solution)/shard_map/while/body/eval_jaxpr/reduce_sum | solution.py:25
  371.3 11.7 %add_reduce_fusion.6 = (bf16[128,128,128]{2,1,0:T(8,128)(2,1)S(1)}, bf16[128,128,128]{2,1,0:T(8,128)(2,1)}) fusion(f32[2,128,128]{2,1,0:T(8,128)S(1)} %get-tuple-element.564, f32[2,128,128]{2,1,0:T(8,128)S(1)} %get-tuple-element.566, f32[2,128,128]{2,1,0:T(8,128)S(1)} %get-tuple-element.567, f32[2,128,128]{2,1,0:T(8,128)S(1)} %get-tuple-element.568), kind=kLoop, calls=%fused_computation.3.clone.1 | loop fusion | flops 29360128 | bytes 8912896 | tf_op jit(solution)/shard_map/while/body/eval_jaxpr/reduce_sum | solution.py:25
  401.0 11.7 %add_reduce_fusion.6 = (bf16[128,128,128]{2,1,0:T(8,128)(2,1)S(1)}, bf16[128,128,128]{2,1,0:T(8,128)(2,1)}) fusion(f32[2,128,128]{2,1,0:T(8,128)S(1)} %get-tuple-element.564, f32[2,128,128]{2,1,0:T(8,128)S(1)} %get-tuple-element.566, f32[2,128,128]{2,1,0:T(8,128)S(1)} %get-tuple-element.567, f32[2,128,128]{2,1,0:T(8,128)S(1)} %get-tuple-element.568), kind=kLoop, calls=%fused_computation.3.clone.1 | loop fusion | flops 29360128 | bytes 8912896 | tf_op jit(solution)/shard_map/while/body/eval_jaxpr/reduce_sum | solution.py:25
  430.6 11.7 %add_reduce_fusion.6 = (bf16[128,128,128]{2,1,0:T(8,128)(2,1)S(1)}, bf16[128,128,128]{2,1,0:T(8,128)(2,1)}) fusion(f32[2,128,128]{2,1,0:T(8,128)S(1)} %get-tuple-element.564, f32[2,128,128]{2,1,0:T(8,128)S(1)} %get-tuple-element.566, f32[2,128,128]{2,1,0:T(8,128)S(1)} %get-tuple-element.567, f32[2,128,128]{2,1,0:T(8,128)S(1)} %get-tuple-element.568), kind=kLoop, calls=%fused_computation.3.clone.1 | loop fusion | flops 29360128 | bytes 8912896 | tf_op jit(solution)/shard_map/while/body/eval_jaxpr/reduce_sum | solution.py:25
  462.1 244.2 %while.41 = (s32[]{:T(128)}, f32[64,16384]{1,0:T(8,128)}, s32[8]{0:T(128)S(1)}, s32[]{:T(128)}, bf16[2,2,128,1024]{3,2,1,0:T(8,128)(2,1)}, /*index=5*/bf16[2,2,1...) while((s32[]{:T(128)}, f32[64,16384]{1,0:T(8,128)}, s32[8]{0:T(128)S(1)}, ...), condition=%wide.region_7.9_spmd.clone, body=%wide.region_4.8_spmd.clone.sunk | while | flops 585442176 | bytes 44893884 | solution.py:62
  464.7 11.7 %add_reduce_fusion.7 = (bf16[128,128,128]{2,1,0:T(8,128)(2,1)S(1)}, bf16[128,128,128]{2,1,0:T(8,128)(2,1)}) fusion(f32[2,128,128]{2,1,0:T(8,128)S(1)} %get-tuple-element.580, f32[2,128,128]{2,1,0:T(8,128)S(1)} %get-tuple-element.582, f32[2,128,128]{2,1,0:T(8,128)S(1)} %get-tuple-element.583, f32[2,128,128]{2,1,0:T(8,128)S(1)} %get-tuple-element.584), kind=kLoop, calls=%fused_computation.34.clone.1 | loop fusion | flops 29360128 | bytes 8912896 | tf_op jit(solution)/shard_map/while/body/eval_jaxpr/reduce_sum | solution.py:25
  494.1 11.7 %add_reduce_fusion.7 = (bf16[128,128,128]{2,1,0:T(8,128)(2,1)S(1)}, bf16[128,128,128]{2,1,0:T(8,128)(2,1)}) fusion(f32[2,128,128]{2,1,0:T(8,128)S(1)} %get-tuple-element.580, f32[2,128,128]{2,1,0:T(8,128)S(1)} %get-tuple-element.582, f32[2,128,128]{2,1,0:T(8,128)S(1)} %get-tuple-element.583, f32[2,128,128]{2,1,0:T(8,128)S(1)} %get-tuple-element.584), kind=kLoop, calls=%fused_computation.34.clone.1 | loop fusion | flops 29360128 | bytes 8912896 | tf_op jit(solution)/shard_map/while/body/eval_jaxpr/reduce_sum | solution.py:25
  524.8 11.7 %add_reduce_fusion.7 = (bf16[128,128,128]{2,1,0:T(8,128)(2,1)S(1)}, bf16[128,128,128]{2,1,0:T(8,128)(2,1)}) fusion(f32[2,128,128]{2,1,0:T(8,128)S(1)} %get-tuple-element.580, f32[2,128,128]{2,1,0:T(8,128)S(1)} %get-tuple-element.582, f32[2,128,128]{2,1,0:T(8,128)S(1)} %get-tuple-element.583, f32[2,128,128]{2,1,0:T(8,128)S(1)} %get-tuple-element.584), kind=kLoop, calls=%fused_computation.34.clone.1 | loop fusion | flops 29360128 | bytes 8912896 | tf_op jit(solution)/shard_map/while/body/eval_jaxpr/reduce_sum | solution.py:25
  555.4 11.7 %add_reduce_fusion.7 = (bf16[128,128,128]{2,1,0:T(8,128)(2,1)S(1)}, bf16[128,128,128]{2,1,0:T(8,128)(2,1)}) fusion(f32[2,128,128]{2,1,0:T(8,128)S(1)} %get-tuple-element.580, f32[2,128,128]{2,1,0:T(8,128)S(1)} %get-tuple-element.582, f32[2,128,128]{2,1,0:T(8,128)S(1)} %get-tuple-element.583, f32[2,128,128]{2,1,0:T(8,128)S(1)} %get-tuple-element.584), kind=kLoop, calls=%fused_computation.34.clone.1 | loop fusion | flops 29360128 | bytes 8912896 | tf_op jit(solution)/shard_map/while/body/eval_jaxpr/reduce_sum | solution.py:25
  586.1 11.7 %add_reduce_fusion.7 = (bf16[128,128,128]{2,1,0:T(8,128)(2,1)S(1)}, bf16[128,128,128]{2,1,0:T(8,128)(2,1)}) fusion(f32[2,128,128]{2,1,0:T(8,128)S(1)} %get-tuple-element.580, f32[2,128,128]{2,1,0:T(8,128)S(1)} %get-tuple-element.582, f32[2,128,128]{2,1,0:T(8,128)S(1)} %get-tuple-element.583, f32[2,128,128]{2,1,0:T(8,128)S(1)} %get-tuple-element.584), kind=kLoop, calls=%fused_computation.34.clone.1 | loop fusion | flops 29360128 | bytes 8912896 | tf_op jit(solution)/shard_map/while/body/eval_jaxpr/reduce_sum | solution.py:25
  647.4 11.7 %add_reduce_fusion.7 = (bf16[128,128,128]{2,1,0:T(8,128)(2,1)S(1)}, bf16[128,128,128]{2,1,0:T(8,128)(2,1)}) fusion(f32[2,128,128]{2,1,0:T(8,128)S(1)} %get-tuple-element.580, f32[2,128,128]{2,1,0:T(8,128)S(1)} %get-tuple-element.582, f32[2,128,128]{2,1,0:T(8,128)S(1)} %get-tuple-element.583, f32[2,128,128]{2,1,0:T(8,128)S(1)} %get-tuple-element.584), kind=kLoop, calls=%fused_computation.34.clone.1 | loop fusion | flops 29360128 | bytes 8912896 | tf_op jit(solution)/shard_map/while/body/eval_jaxpr/reduce_sum | solution.py:25
  678.0 11.7 %add_reduce_fusion.7 = (bf16[128,128,128]{2,1,0:T(8,128)(2,1)S(1)}, bf16[128,128,128]{2,1,0:T(8,128)(2,1)}) fusion(f32[2,128,128]{2,1,0:T(8,128)S(1)} %get-tuple-element.580, f32[2,128,128]{2,1,0:T(8,128)S(1)} %get-tuple-element.582, f32[2,128,128]{2,1,0:T(8,128)S(1)} %get-tuple-element.583, f32[2,128,128]{2,1,0:T(8,128)S(1)} %get-tuple-element.584), kind=kLoop, calls=%fused_computation.34.clone.1 | loop fusion | flops 29360128 | bytes 8912896 | tf_op jit(solution)/shard_map/while/body/eval_jaxpr/reduce_sum | solution.py:25
  711.0 243.4 %while.42 = (s32[]{:T(128)}, f32[64,16384]{1,0:T(8,128)}, s32[8]{0:T(128)S(1)}, s32[]{:T(128)}, bf16[2,2,128,1024]{3,2,1,0:T(8,128)(2,1)}, /*index=5*/bf16[2,2,1...) while((s32[]{:T(128)}, f32[64,16384]{1,0:T(8,128)}, s32[8]{0:T(128)S(1)}, ...), condition=%wide.region_11.13_spmd.clone, body=%wide.region_8.12_spmd.clone.sunk | while | flops 585442176 | bytes 44893884 | solution.py:62
  742.7 11.7 %add_reduce_fusion.8 = (bf16[128,128,128]{2,1,0:T(8,128)(2,1)S(1)}, bf16[128,128,128]{2,1,0:T(8,128)(2,1)}) fusion(f32[2,128,128]{2,1,0:T(8,128)S(1)} %get-tuple-element.596, f32[2,128,128]{2,1,0:T(8,128)S(1)} %get-tuple-element.598, f32[2,128,128]{2,1,0:T(8,128)S(1)} %get-tuple-element.599, f32[2,128,128]{2,1,0:T(8,128)S(1)} %get-tuple-element.600), kind=kLoop, calls=%fused_computation.65.clone.1 | loop fusion | flops 29360128 | bytes 8912896 | tf_op jit(solution)/shard_map/while/body/eval_jaxpr/reduce_sum | solution.py:25
  773.3 11.7 %add_reduce_fusion.8 = (bf16[128,128,128]{2,1,0:T(8,128)(2,1)S(1)}, bf16[128,128,128]{2,1,0:T(8,128)(2,1)}) fusion(f32[2,128,128]{2,1,0:T(8,128)S(1)} %get-tuple-element.596, f32[2,128,128]{2,1,0:T(8,128)S(1)} %get-tuple-element.598, f32[2,128,128]{2,1,0:T(8,128)S(1)} %get-tuple-element.599, f32[2,128,128]{2,1,0:T(8,128)S(1)} %get-tuple-element.600), kind=kLoop, calls=%fused_computation.65.clone.1 | loop fusion | flops 29360128 | bytes 8912896 | tf_op jit(solution)/shard_map/while/body/eval_jaxpr/reduce_sum | solution.py:25
  803.9 11.7 %add_reduce_fusion.8 = (bf16[128,128,128]{2,1,0:T(8,128)(2,1)S(1)}, bf16[128,128,128]{2,1,0:T(8,128)(2,1)}) fusion(f32[2,128,128]{2,1,0:T(8,128)S(1)} %get-tuple-element.596, f32[2,128,128]{2,1,0:T(8,128)S(1)} %get-tuple-element.598, f32[2,128,128]{2,1,0:T(8,128)S(1)} %get-tuple-element.599, f32[2,128,128]{2,1,0:T(8,128)S(1)} %get-tuple-element.600), kind=kLoop, calls=%fused_computation.65.clone.1 | loop fusion | flops 29360128 | bytes 8912896 | tf_op jit(solution)/shard_map/while/body/eval_jaxpr/reduce_sum | solution.py:25
  834.4 11.7 %add_reduce_fusion.8 = (bf16[128,128,128]{2,1,0:T(8,128)(2,1)S(1)}, bf16[128,128,128]{2,1,0:T(8,128)(2,1)}) fusion(f32[2,128,128]{2,1,0:T(8,128)S(1)} %get-tuple-element.596, f32[2,128,128]{2,1,0:T(8,128)S(1)} %get-tuple-element.598, f32[2,128,128]{2,1,0:T(8,128)S(1)} %get-tuple-element.599, f32[2,128,128]{2,1,0:T(8,128)S(1)} %get-tuple-element.600), kind=kLoop, calls=%fused_computation.65.clone.1 | loop fusion | flops 29360128 | bytes 8912896 | tf_op jit(solution)/shard_map/while/body/eval_jaxpr/reduce_sum | solution.py:25
  865.0 11.7 %add_reduce_fusion.8 = (bf16[128,128,128]{2,1,0:T(8,128)(2,1)S(1)}, bf16[128,128,128]{2,1,0:T(8,128)(2,1)}) fusion(f32[2,128,128]{2,1,0:T(8,128)S(1)} %get-tuple-element.596, f32[2,128,128]{2,1,0:T(8,128)S(1)} %get-tuple-element.598, f32[2,128,128]{2,1,0:T(8,128)S(1)} %get-tuple-element.599, f32[2,128,128]{2,1,0:T(8,128)S(1)} %get-tuple-element.600), kind=kLoop, calls=%fused_computation.65.clone.1 | loop fusion | flops 29360128 | bytes 8912896 | tf_op jit(solution)/shard_map/while/body/eval_jaxpr/reduce_sum | solution.py:25
  968.6 41.2 %reduce-scatter.5.cloned.1.call-done = bf16[8,49152]{1,0:T(8,128)(2,1)} async-done(((bf16[64,49152]{1,0:T(8,128)(2,1)}), bf16[8,49152]{1,0:T(8,128)(2,1)}) %reduce-scatter.5.cloned.1.call-update) | async-done | bytes 786448
  (301 shorter events, 527.0 us)
Async XLA Ops:
  6.5 203.4 %all-gather.2.cloned.1.call-start = ((), (), s32[]{:S(2)}) async-start(), calls=%async_computation.1 | async-start | bytes 35651584 | tf_op jit(solution)/shard_map/all_gather | solution.py:71
  7.3 1002.6 %reduce-scatter.5.cloned.1.call-start = ((), (), s32[]{:S(2)}) async-start(), calls=%async_computation.2 | async-start | bytes 7077888
  954.4 3.5 copy-start
Sparse Core Ops, SparseCore 0:
  9.5 200.4 all-gather.1
  968.8 41.0 reduce-scatter.4
where the time goes:
time: 1020 us
  other arithmetic  475 us (47%)
  waiting for transfers between devices  229 us (22%)
  matrix products  218 us (21%)
  local copies, waits for them, and re-layouts  54.9 us (5%)
  between operations  25.5 us (2%)
  loops' own time  16.6 us (2%)
    reduce_sum x24, other arithmetic, cross_block(): jnp.sum(left_wide[:, 0, :, None, :] * right_wide[:, 0, None, :, :] + left...  280 us
    dot_general x24, matrix products, block_step(): lax.dot_general(phases, stacked, (((0,), (1,)), ((), ())), preferred_elem...  218 us
    all_gather x1, waiting for transfers between devices, per_device(): shards = lax.all_gather(spectra, 'tiles', axis=0, tiled=True)  187 us
    concatenate x24, other arithmetic, cross_block(): jnp.concatenate([real_part, imag_part], axis=-1)  171 us
    unnamed x3, waiting for transfers between devices  42 us
  transfers between devices with their start and end apart: 2, of which 2 were waited for; matrix products, arithmetic and copies ran while one was open for 0% of the time, Pallas kernels for 0%

commit v1 on v0

v1 whole, which is shorter than its diff:
```python
import math

import jax
import jax.numpy as jnp
from jax import lax
from jax.experimental import pallas as pl
from jax.experimental.pallas import tpu as pltpu
from jax.sharding import PartitionSpec as P

F = 8192
W = 2
LAGS = 64
CH = 128
T1 = 8
T0 = 8
KC = 256


def phase_tables(first, width):
    freqs = first + jnp.arange(width, dtype=jnp.int32)
    coarse = T0 * jnp.arange(T1, dtype=jnp.int32) - LAGS // 2
    fine = -jnp.arange(T0, dtype=jnp.int32)

    def table(shifts):
        index = (freqs[None, :] * (shifts % F)[:, None]) % F
        angles = index.astype(jnp.float32) * (2.0 * math.pi / F)
        return jnp.stack([jnp.cos(angles), jnp.sin(angles)], axis=1)

    return table(coarse), table(fine)


def rotate(ref, window, table, count, dst, base):
    real = ref[window, 0].astype(jnp.float32)
    imag = ref[window, 1].astype(jnp.float32)
    for t in range(count):
        c = table[t, 0:1, :]
        s = table[t, 1:2, :]
        dst[t * CH : (t + 1) * CH, base : base + KC] = (real * c - imag * s).astype(jnp.bfloat16)
        dst[t * CH : (t + 1) * CH, base + KC : base + 2 * KC] = (real * s + imag * c).astype(
            jnp.bfloat16
        )


def pair_kernel(ids, a_ref, b_ref, coarse_ref, fine_ref, o_ref, u, v, acc):
    step = pl.program_id(1)

    @pl.when(step == 0)
    def _():
        acc[...] = jnp.zeros_like(acc)

    for w in range(W):
        rotate(a_ref, w, coarse_ref, T1, u, w * 2 * KC)
        rotate(b_ref, w, fine_ref, T0, v, w * 2 * KC)
    acc[...] += lax.dot_general(
        u[...], v[...], (((1,), (1,)), ((), ())), preferred_element_type=jnp.float32
    )

    @pl.when(step == pl.num_programs(1) - 1)
    def _():
        norm = 1.0 / math.sqrt(2.0 * W * F)
        for i in range(T1):
            for j in range(T0):
                block = acc[i * CH : (i + 1) * CH, j * CH : (j + 1) * CH]
                o_ref[i * T0 + j] = (block * norm).astype(jnp.bfloat16)


def pair_tiles(blocks, ids, coarse, fine):
    slots = ids.shape[0] // 2
    width = blocks.shape[-1]
    block = (None, W, 2, CH, KC)
    table = pl.BlockSpec((T1, 2, KC), lambda s, k, ids: (0, 0, k))
    grid_spec = pltpu.PrefetchScalarGridSpec(
        num_scalar_prefetch=1,
        grid=(slots, width // KC),
        in_specs=[
            pl.BlockSpec(block, lambda s, k, ids: (ids[2 * s], 0, 0, 0, k)),
            pl.BlockSpec(block, lambda s, k, ids: (ids[2 * s + 1], 0, 0, 0, k)),
            table,
            table,
        ],
        out_specs=pl.BlockSpec((None, LAGS, CH, CH), lambda s, k, ids: (s, 0, 0, 0)),
        scratch_shapes=[
            pltpu.VMEM((T1 * CH, 2 * W * KC), jnp.bfloat16),
            pltpu.VMEM((T0 * CH, 2 * W * KC), jnp.bfloat16),
            pltpu.VMEM((T1 * CH, T0 * CH), jnp.float32),
        ],
    )
    return pl.pallas_call(
        pair_kernel,
        grid_spec=grid_spec,
        out_shape=jax.ShapeDtypeStruct((slots, LAGS, CH, CH), jnp.bfloat16),
        name="pair_tiles",
    )(ids, blocks, blocks, coarse, fine)


def per_device(spectra, requests, pairs, counts):
    width = spectra.shape[-1]
    wanted = lax.dynamic_index_in_dim(requests, lax.axis_index("tiles"), 0, keepdims=False)
    shards = lax.all_gather(spectra, "tiles", axis=0, tiled=True)
    ids = wanted[pairs[0].reshape(-1)]
    coarse, fine = phase_tables(lax.axis_index("lag") * width, width)
    partial = pair_tiles(shards, ids, coarse, fine)
    live = jnp.arange(partial.shape[0]) < counts[0]
    summed = lax.psum_scatter(partial, "lag", scatter_dimension=1, tiled=True)
    return jnp.where(live[:, None, None, None], summed.astype(jnp.float32), 0.0)


def solution(mesh):
    placed = (P("tiles", None, None, None, "lag"), P(), P("tiles", None, None), P("tiles"))
    return jax.shard_map(
        per_device,
        mesh=mesh,
        in_specs=placed,
        out_specs=P("tiles", "lag", None, None),
        check_vma=False,
    )
```

time: 1020 us -> 307 us (0.30)
  other arithmetic: 475 us -> 4.85 us
  matrix products: 218 us -> 0 us
  local copies, waits for them, and re-layouts: 54.9 us -> 13.8 us
  Pallas kernels: 0 us -> 34.3 us
  loops' own time: 16.6 us -> 0 us
  between operations: 25.5 us -> 14.1 us
    reduce_sum x24 -> x0, other arithmetic: 280 us -> none  [cross_block(): jnp.sum(left_wide[:, 0, :, None, :] * right_wide[:, 0, None, :, :] + left...]
    dot_general x24 -> x0, matrix products: 218 us -> none  [block_step(): lax.dot_general(phases, stacked, (((0,), (1,)), ((), ())), preferred_elem...]
    concatenate x24 -> x0, other arithmetic: 171 us -> none  [cross_block(): jnp.concatenate([real_part, imag_part], axis=-1)]
    pallas_call x0 -> x1, Pallas kernels: none -> 34.3 us  [pair_tiles(): pl.pallas_call(pair_kernel, grid_spec=grid_spec, out_shape=jax.ShapeDtype...]
    dynamic_slice x48 -> x1, local copies, waits for them, and re-layouts: 31.5 us -> 0.18 us  [per_device(): lax.dynamic_index_in_dim(requests, lax.axis_index('tiles'), 0, keepdims=F...]
    another operation x3 -> x0, loops' own time: 16.6 us -> none  [band_sum(): lax.scan(block_step, running, jnp.arange(block_count, dtype=jnp.int32))]
    all_gather x1, waiting for transfers between devices: 187 us -> 198 us  [per_device(): shards = lax.all_gather(spectra, 'tiles', axis=0, tiled=True)]
  transfers between devices with their start and end apart: 2 -> 2, of which waited for: 2 -> 2; matrix products, arithmetic and copies ran while one was open for 0% -> 2% of each run, Pallas kernels for 0% -> 0%
where the time goes in v1:
time: 307 us; the launch traced here: 306 us
  waiting for transfers between devices  239 us (78%)
  Pallas kernels  34.3 us (11%)
  between operations  14.1 us (5%)
  local copies, waits for them, and re-layouts  13.8 us (4%)
  other arithmetic  4.85 us (2%)
    all_gather x1, waiting for transfers between devices, per_device(): shards = lax.all_gather(spectra, 'tiles', axis=0, tiled=True)  198 us
    unnamed x3, waiting for transfers between devices  41.7 us
    pallas_call x1, Pallas kernels, pair_tiles(): pl.pallas_call(pair_kernel, grid_spec=grid_spec, out_shape=jax.ShapeDtype...  34.3 us
    unnamed x8, local copies, waits for them, and re-layouts  12.4 us
  transfers between devices with their start and end apart: 2, of which 2 were waited for; matrix products, arithmetic and copies ran while one was open for 2% of the time, Pallas kernels for 0%

profile of v1, /device:TPU:1, one launch (start us, length us, event | category | flops | bytes accessed | tf_op | source)
XLA Modules:
  0.0 306.5 jit_solution(2450349374455513357)
XLA Ops:
  6.5 0.0 copy-start
  6.5 0.0 copy-start.1
  6.5 0.0 all-gather.2.cloned.1.call-start
  6.5 0.7 all-gather.2.cloned.1.call-update
  7.3 0.0 reduce-scatter.5.cloned.1.call-start
  7.3 0.0 copy-done.1
  7.3 0.1 copy.8
  7.4 0.1 reshape_squeeze.3
  7.5 0.0 copy-done
  7.5 0.2 dynamic-slice_reduce_fusion
  7.7 1.2 gather_fusion
  8.9 0.1 fusion.1
  9.0 1.9 fusion.5
  11.0 0.7 pad_maximum_fusion.1.fine_ref
  11.6 0.7 pad_maximum_fusion.coarse_ref
  12.3 197.6 %all-gather.2.cloned.1.call-done.a_ref.b_ref = bf16[32,2,2,128,1024]{4,3,2,1,0:T(8,128)(2,1)} async-done(((bf16[2,2,2,128,1024]{4,3,2,1,0:T(8,128)(2,1)}), bf16[32,2,2,128,1024]{4,3,2,1,0:T(8,128)(2,1)}) %all-gather.2.cloned.1.call-update) | async-done | bytes 33554448 | tf_op jit(solution)/shard_map/all_gather | solution.py:99
  210.0 34.3 %pair_tiles.1 = bf16[3,64,128,128]{3,2,1,0:T(8,128)(2,1)} custom-call(s32[6]{0:T(128)} %gather_fusion, bf16[32,2,2,128,1024]{4,3,2,1,0:T(8,128)(2,1)} %all-gather.2.cloned.1.call-done.a_ref.b_ref, bf16[32,2,2,128,1024]{4,3,2,1,0:T(8,128)(2,1)} %all-gather.2.cloned.1.call-done.a_ref.b_ref, f32[8,2,1024]{2,1,0:T(2,128)} %pad_maximum_fusion.coarse_ref, ...), custom_call_target="tpu_custom_call" | custom-call | tf_op jit(solution)/shard_map/pair_tiles/pallas_call | solution.py:88
  244.3 4.1 %copy.11 = bf16[3,64,128,128]{3,2,0,1:T(8,128)(2,1)S(1)} copy(bf16[3,64,128,128]{3,2,1,0:T(8,128)(2,1)} %pair_tiles.1) | data formatting | bytes 12582912
  248.4 6.9 %copy.27 = bf16[8,8,384,128]{3,1,2,0:T(8,128)(2,1)} copy(bf16[8,8,384,128]{3,2,1,0:T(8,128)(2,1)S(1)} %bitcast.18) | data formatting | bytes 12582912
  255.3 0.0 reduce-scatter.5.cloned.1.call-update
  256.0 41.0 %reduce-scatter.5.cloned.1.call-done = bf16[8,49152]{1,0:T(8,128)(2,1)} async-done(((bf16[64,49152]{1,0:T(8,128)(2,1)}), bf16[8,49152]{1,0:T(8,128)(2,1)}) %reduce-scatter.5.cloned.1.call-update) | async-done | bytes 786448
  297.0 1.2 copy.14
  298.3 1.4 convert_select_fusion
  (6 shorter events, 0.0 us)
Async XLA Ops:
  6.5 1.0 copy-start
  6.5 0.8 copy-start.1
  6.5 203.4 %all-gather.2.cloned.1.call-start = ((), (), s32[]{:S(2)}) async-start(), calls=%async_computation.1 | async-start | bytes 35651584 | tf_op jit(solution)/shard_map/all_gather | solution.py:99
  7.3 289.8 %reduce-scatter.5.cloned.1.call-start = ((), (), s32[]{:S(2)}) async-start(), calls=%async_computation.2 | async-start | bytes 7077888
Sparse Core Ops, SparseCore 0:
  9.5 200.4 all-gather.1
  255.5 41.4 reduce-scatter.4

commit v2 on v1

v2 whole, which is shorter than its diff:
```python
import math

import jax
import jax.numpy as jnp
import numpy as np
from jax import lax
from jax.experimental import pallas as pl
from jax.experimental.pallas import tpu as pltpu
from jax.sharding import PartitionSpec as P

MESH = pl.DeviceIdType.MESH
F = 8192
W = 2
LAGS = 64
CH = 128
BAND = 1024
NEED = 6
SLOTS = 3
SIDE = 4
T1 = 8
T0 = 8
CHUNKS = 4
KC = BAND // CHUNKS
NORM = 1.0 / math.sqrt(2.0 * W * F)


def phase_tables():
    freqs = np.arange(F, dtype=np.int64)
    coarse = T0 * np.arange(T1) - LAGS // 2
    fine = -np.arange(T0)

    def table(shifts):
        angles = (freqs[None, :] * shifts[:, None] % F) * (2.0 * math.pi / F)
        both = np.stack([np.cos(angles), np.sin(angles)], axis=1).astype(np.float32)
        return both.reshape(8, 2, F // BAND, BAND).transpose(2, 0, 1, 3)

    return np.stack([table(coarse), table(fine)], axis=1)


def pick(flags, values):
    total = jnp.int32(0)
    for flag, value in zip(flags, values, strict=True):
        total = total + jnp.where(flag, value, 0)
    return total


def request_plan(req_ref, node, along, across, by_y):
    rel, index = [], []
    for q in range(NEED):
        block = req_ref[node, q]
        holder = lax.div(block, 2)
        hy, hz = lax.div(holder, SIDE), lax.rem(holder, SIDE)
        h_along, h_across = (hy, hz) if by_y else (hz, hy)
        rel.append(lax.rem(h_along - along + SIDE, SIDE))
        index.append(2 * lax.rem(h_across - across + SIDE, SIDE) + lax.rem(block, 2))
    rank = []
    for q in range(NEED):
        total = jnp.int32(0)
        for earlier in range(q):
            total = total + jnp.where(rel[earlier] == rel[q], 1, 0)
        rank.append(total)
    n1 = pick([r == 1 for r in rel], [1] * NEED)
    n2 = pick([r == 2 for r in rel], [1] * NEED)
    plus = jnp.minimum(jnp.minimum(n2, 2), 4 - n1)
    return rel, index, rank, plus, n2 - plus


def kernel(*args):
    req_ref, pairs_ref, x_hbm, tab_hbm, o_ref = args[:5]
    rest = list(args[5:])

    def take(count):
        taken, rest[:count] = rest[:count], []
        return taken

    R = [take(CHUNKS) for _ in range(W)]
    FR = [take(CHUNKS) for _ in range(W)]
    TR = [take(CHUNKS) for _ in range(W)]
    FS = [take(2) for _ in range(W)]
    TS = [take(2) for _ in range(W)]
    tab, ab, u, v, acc, loc = take(6)
    PS, PR, S, XR, XS, YR = (take(SLOTS) for _ in range(6))
    local_sem, tab_sem, s1, r1, s1b, r1b, st, rt, sf, rf, sp, rp, sx, rx = take(14)

    me, lag = lax.axis_index("tiles"), lax.axis_index("lag")
    y, z = lax.div(me, SIDE), lax.rem(me, SIDE)
    x, core = lax.div(lag, 2), lax.rem(lag, 2)

    def shift(a, by):
        return lax.rem(a + by + SIDE, SIDE)

    def at(by_y, by):
        return (shift(y, by) * SIDE + z, lag) if by_y else (y * SIDE + shift(z, by), lag)

    def along_x(by):
        return (me, shift(x, by) * 2 + core)

    partner = (me, 2 * x + 1 - core)

    tables = pltpu.make_async_copy(tab_hbm.at[lag], tab, tab_sem)
    loads = {}
    for c in range(CHUNKS):
        for w in range(W):
            loads[c, w] = pltpu.make_async_copy(
                x_hbm.at[:, w, :, :, pl.ds(c * KC, KC)], R[w][c].at[0:2], local_sem.at[c, w]
            )
            loads[c, w].start()
    tables.start()
    barrier = pltpu.get_barrier_semaphore()
    friends = [at(True, -1), at(True, 1), at(False, -1), at(False, 1)]
    friends += [along_x(-1), along_x(1), partner]
    for friend in friends:
        pl.semaphore_signal(barrier, inc=1, device_id=friend, device_id_type=MESH)
    pl.semaphore_wait(barrier, len(friends))

    def remote(src, dst, send, recv, to):
        copy = pltpu.make_async_remote_copy(
            src_ref=src, dst_ref=dst, send_sem=send, recv_sem=recv, device_id=to, device_id_type=MESH
        )
        copy.start()
        return copy

    first, second, transit, final = {}, {}, {}, {}

    def start_first(c):
        for w in range(W):
            loads[c, w].wait()
            for k, (by, slot) in enumerate(((-1, 1), (1, 3))):
                for b in (k, 1 - k):
                    first[c, w, k, b] = remote(
                        R[w][c].at[b],
                        R[w][c].at[2 * slot + b],
                        s1.at[c, w, k, b],
                        r1.at[c, w, k, b],
                        at(w == 1, by),
                    )

    def start_second(c):
        for w in range(W):
            for k, (by, slot) in enumerate(((-1, 1), (1, 3))):
                first[c, w, k, k].wait_recv()
                second[c, w, k] = remote(
                    R[w][c].at[2 * slot + k],
                    R[w][c].at[4 + k],
                    s1b.at[c, w, k],
                    r1b.at[c, w, k],
                    at(w == 1, by),
                )

    start_first(0)
    start_first(1)

    finals, transits, passing = {}, {}, {}
    for w in range(W):
        along, across = (y, z) if w == 0 else (z, y)
        by_y = w == 0

        def plan(by):
            there = shift(along, by)
            node = there * SIDE + across if by_y else across * SIDE + there
            return request_plan(req_ref, node, there, across, by_y)

        for k, (by, mine) in enumerate(((-1, 1), (1, 3))):
            rel, index, rank, plus, minus = plan(by)
            for j in range(4):
                finals[w, k, j] = pick(
                    [(a == mine) & (b == j) for a, b in zip(rel, rank, strict=True)], index
                )
            passing[w, k] = (plus, minus)[k]
        rel, index, rank, plus, minus = plan(2)
        for j in range(2):
            transits[w, 0, j] = pick(
                [(a == 2) & (b < plus) & (b == j) for a, b in zip(rel, rank, strict=True)], index
            )
            transits[w, 1, j] = pick(
                [(a == 2) & (b - plus == j) for a, b in zip(rel, rank, strict=True)], index
            )
        rel, index, rank, plus, minus = plan(0)
        for q in range(NEED):
            r = rank[q]
            far = jnp.where(r < plus, 8 + 3 - r, 12 + 3 - (r - plus))
            where = jnp.where(rel[q] == 2, far, jnp.where(rel[q] == 3, 12 + r, 8 + r))
            loc[w, q] = jnp.where(rel[q] == 0, index[q], where)

    def start_third(c):
        half = c % 2
        if c >= 2:
            for w in range(W):
                for k in range(2):
                    transit[c - 2, w, k].wait_send()
                    final[c - 2, w, k, 0].wait_send()
                    final[c - 2, w, k, 1].wait_send()
        for w in range(W):
            for k in range(2):
                first[c, w, k, 1 - k].wait_recv()
                second[c, w, k].wait_recv()
        for w in range(W):
            for k in range(2):
                for j in range(2):
                    TS[w][half][k, j] = R[w][c][transits[w, k, j]]
        for w in range(W):
            for k, by in enumerate((-1, 1)):
                transit[c, w, k] = remote(
                    TS[w][half].at[k], TR[w][c].at[k], st.at[c, w, k], rt.at[c, w, k], at(w == 0, by)
                )
        for w in range(W):
            for k in range(2):
                for j in range(2):
                    FS[w][half][k, j] = R[w][c][finals[w, k, j]]
        for w in range(W):
            for k, by in enumerate((-1, 1)):
                final[c, w, k, 0] = remote(
                    FS[w][half].at[k, 0:2],
                    FR[w][c].at[4 * k : 4 * k + 2],
                    sf.at[c, w, k, 0],
                    rf.at[c, w, k, 0],
                    at(w == 0, by),
                )

    def start_fourth(c):
        half = c % 2
        for w in range(W):
            for k in range(2):
                transit[c, w, k].wait_recv()
        for w in range(W):
            for k in range(2):
                for j in (2, 3):
                    direct = R[w][c][finals[w, k, j]]
                    passed = TR[w][c][k, 3 - j]
                    FS[w][half][k, j] = jnp.where(passing[w, k] > 3 - j, passed, direct)
        for w in range(W):
            for k, by in enumerate((-1, 1)):
                final[c, w, k, 1] = remote(
                    FS[w][half].at[k, 2:4],
                    FR[w][c].at[4 * k + 2 : 4 * k + 4],
                    sf.at[c, w, k, 1],
                    rf.at[c, w, k, 1],
                    at(w == 0, by),
                )

    def wait_finals(c):
        for w in range(W):
            for k in range(2):
                final[c, w, k, 0].wait_recv()
                final[c, w, k, 1].wait_recv()

    def compute(c, s):
        for w in range(W):
            for side in range(2):
                where = loc[w, pairs_ref[0, s, side]]
                i = lax.rem(where, 8)
                block = jnp.where(where < 8, R[w][c][i], FR[w][c][i])
                ab[side, w] = block.astype(jnp.float32)

        def rotate(t, carry):
            rows = pl.ds(pl.multiple_of(t * CH, CH), CH)
            for side, dst in enumerate((u, v)):
                cos = tab[side, t, 0:1, c * KC : (c + 1) * KC]
                sin = tab[side, t, 1:2, c * KC : (c + 1) * KC]
                for w in range(W):
                    real, imag = ab[side, w, 0], ab[side, w, 1]
                    base = 2 * w * KC
                    dst[rows, base : base + KC] = (real * cos - imag * sin).astype(jnp.bfloat16)
                    dst[rows, base + KC : base + 2 * KC] = (real * sin + imag * cos).astype(
                        jnp.bfloat16
                    )
            return carry

        lax.fori_loop(0, T1, rotate, 0)

        def multiply(n, carry):
            cols = pl.ds(pl.multiple_of(n * 256, 256), 256)
            part = lax.dot_general(
                u[...], v[cols, :], (((1,), (1,)), ((), ())), preferred_element_type=jnp.float32
            )
            if c == 0:
                acc[s, :, cols] = part
            else:
                acc[s, :, cols] += part
            return carry

        lax.fori_loop(0, T0 * CH // 256, multiply, 0)

    def compute_all(c):
        def one(s, carry):
            compute(c, s)
            return carry

        lax.fori_loop(0, SLOTS, one, 0)

    pair_copy, x_copy = {}, {}

    def rows_of(there, which):
        return pl.ds(pl.multiple_of((2 * there + which) * CH, CH), CH)

    def send_pair(s):
        for there in range(SIDE):
            PS[s][there] = (acc[s, rows_of(there, 1 - core), :] * NORM).astype(jnp.bfloat16)
        pair_copy[s] = remote(PS[s], PR[s], sp.at[s], rp.at[s], partner)

    HALF = T0 * CH // 2
    lo, hi = slice(0, HALF), slice(HALF, 2 * HALF)

    def chip_sum(s):
        pair_copy[s].wait_recv()

        def total(by):
            there = shift(x, by)
            mine = acc[s, rows_of(there, core), :] * NORM
            return mine + PR[s][there].astype(jnp.float32)

        far = total(2).astype(jnp.bfloat16)
        XS[s][0, 0] = far[:, lo]
        XS[s][1, 0] = far[:, hi]
        for k, by in enumerate((1, -1)):
            x_copy[s, k, 0] = remote(
                XS[s].at[k, 0], XR[s].at[k, 0], sx.at[s, k, 0], rx.at[s, k, 0], along_x(by)
            )
        for k, by in enumerate((1, -1)):
            near = total(by)
            relayed, own = (lo, hi) if k == 0 else (hi, lo)
            YR[s][k] = near[:, relayed]
            XS[s][k, 1] = near[:, own].astype(jnp.bfloat16)
            x_copy[s, k, 1] = remote(
                XS[s].at[k, 1], XR[s].at[k, 1], sx.at[s, k, 1], rx.at[s, k, 1], along_x(by)
            )
        S[s][...] = total(0)

    def relay(s):
        for k, by in enumerate((1, -1)):
            x_copy[s, k, 0].wait_recv()
            XS[s][k, 2] = (YR[s][k] + XR[s][k, 0].astype(jnp.float32)).astype(jnp.bfloat16)
            x_copy[s, k, 2] = remote(
                XS[s].at[k, 2], XR[s].at[k, 2], sx.at[s, k, 2], rx.at[s, k, 2], along_x(by)
            )

    def finish(s):
        for k in range(2):
            x_copy[s, k, 1].wait_recv()
            x_copy[s, k, 2].wait_recv()
        low = S[s][:, lo] + XR[s][0, 2].astype(jnp.float32) + XR[s][1, 1].astype(jnp.float32)
        high = S[s][:, hi] + XR[s][0, 1].astype(jnp.float32) + XR[s][1, 2].astype(jnp.float32)
        for t in range(T0 // 2):
            o_ref[s, t] = low[:, t * CH : (t + 1) * CH]
            o_ref[s, T0 // 2 + t] = high[:, t * CH : (t + 1) * CH]

    tables.wait()
    start_second(0)
    start_first(2)
    for c in range(CHUNKS):
        start_third(c)
        start_fourth(c)
        if c + 1 < CHUNKS:
            start_second(c + 1)
        if c + 3 < CHUNKS:
            start_first(c + 3)
        if c > 0:
            wait_finals(c - 1)
            compute_all(c - 1)
    last = CHUNKS - 1
    wait_finals(last)
    compute(last, 0)
    send_pair(0)
    compute(last, 1)
    send_pair(1)
    chip_sum(0)
    compute(last, 2)
    send_pair(2)
    relay(0)
    chip_sum(1)
    relay(1)
    chip_sum(2)
    finish(0)
    relay(2)
    finish(1)
    finish(2)

    for copy in list(first.values()) + list(second.values()):
        copy.wait_send()
    for c in (CHUNKS - 2, CHUNKS - 1):
        for w in range(W):
            for k in range(2):
                transit[c, w, k].wait_send()
                final[c, w, k, 0].wait_send()
                final[c, w, k, 1].wait_send()
    for copy in list(pair_copy.values()) + list(x_copy.values()):
        copy.wait_send()


def per_device(spectra, requests, pairs, counts, tables):
    bf16, f32 = jnp.bfloat16, jnp.float32
    vmem, dma = pltpu.VMEM, pltpu.SemaphoreType.DMA
    half = (2, CH, KC)
    scratch = [vmem((8, *half), bf16)] * (W * CHUNKS)
    scratch += [vmem((8, *half), bf16)] * (W * CHUNKS)
    scratch += [vmem((2, 2, *half), bf16)] * (W * CHUNKS)
    scratch += [vmem((2, 4, *half), bf16)] * (W * 2)
    scratch += [vmem((2, 2, *half), bf16)] * (W * 2)
    scratch += [
        vmem((2, 8, 2, BAND), f32),
        vmem((2, W, 2, CH, KC), f32),
        vmem((T1 * CH, 2 * W * KC), bf16),
        vmem((T0 * CH, 2 * W * KC), bf16),
        vmem((SLOTS, T1 * CH, T0 * CH), f32),
        pltpu.SMEM((W, NEED), jnp.int32),
    ]
    scratch += [vmem((SIDE, CH, T0 * CH), bf16)] * (2 * SLOTS)
    scratch += [vmem((CH, T0 * CH), f32)] * SLOTS
    scratch += [vmem((2, 3, CH, T0 * CH // 2), bf16)] * (2 * SLOTS)
    scratch += [vmem((2, CH, T0 * CH // 2), f32)] * SLOTS
    scratch += [
        dma((CHUNKS, W)),
        dma,
        dma((CHUNKS, W, 2, 2)),
        dma((CHUNKS, W, 2, 2)),
        dma((CHUNKS, W, 2)),
        dma((CHUNKS, W, 2)),
        dma((CHUNKS, W, 2)),
        dma((CHUNKS, W, 2)),
        dma((CHUNKS, W, 2, 2)),
        dma((CHUNKS, W, 2, 2)),
        dma((SLOTS,)),
        dma((SLOTS,)),
        dma((SLOTS, 2, 3)),
        dma((SLOTS, 2, 3)),
    ]
    smem = pl.BlockSpec(memory_space=pltpu.SMEM)
    hbm = pl.BlockSpec(memory_space=pl.ANY)
    summed = pl.pallas_call(
        kernel,
        out_shape=jax.ShapeDtypeStruct((SLOTS, T0, CH, CH), f32),
        in_specs=[smem, smem, hbm, hbm],
        out_specs=pl.BlockSpec(memory_space=pltpu.VMEM),
        scratch_shapes=scratch,
        compiler_params=pltpu.CompilerParams(
            collective_id=0, has_side_effects=True, vmem_limit_bytes=67043328
        ),
        name="correlate",
    )(requests, pairs, spectra, tables)
    live = jnp.arange(SLOTS) < counts[0]
    return jnp.where(live[:, None, None, None], summed, 0.0)


def solution(mesh):
    placed = (P("tiles", None, None, None, "lag"), P(), P("tiles", None, None), P("tiles"), P())
    tables = phase_tables()
    mapped = jax.shard_map(
        per_device,
        mesh=mesh,
        in_specs=placed,
        out_specs=P("tiles", "lag", None, None),
        check_vma=False,
    )

    def run(spectra, requests, pairs, counts):
        return mapped(spectra, requests, pairs, counts, jnp.asarray(tables))

    return run
```

time: 307 us -> 161 us (0.52)
  waiting for transfers between devices: 239 us -> 0 us
  Pallas kernels: 34.3 us -> 155 us
  between operations: 14.1 us -> 0.66 us
  local copies, waits for them, and re-layouts: 13.8 us -> 2.69 us
    all_gather x1 -> x0, waiting for transfers between devices: 198 us -> none  [per_device(): shards = lax.all_gather(spectra, 'tiles', axis=0, tiled=True)]
    pallas_call x1, Pallas kernels: 34.3 us -> 155 us  [per_device(): pl.pallas_call(kernel, out_shape=jax.ShapeDtypeStruct((SLOTS, T0, CH, CH)...]
    unnamed x3 -> x0, waiting for transfers between devices: 41.7 us -> none
    unnamed x8 -> x2, local copies, waits for them, and re-layouts: 12.4 us -> 2.69 us
  transfers between devices with their start and end apart: 2 -> 0, of which waited for: 2 -> 0; matrix products, arithmetic and copies ran while one was open for 2% -> 0% of each run, Pallas kernels for 0% -> 0%
where the time goes in v2:
time: 161 us
  Pallas kernels  155 us (96%)
  other arithmetic  2.8 us (2%)
  local copies, waits for them, and re-layouts  2.69 us (2%)
    pallas_call x1, Pallas kernels, per_device(): pl.pallas_call(kernel, out_shape=jax.ShapeDtypeStruct((SLOTS, T0, CH, CH)...  155 us

profile of v2, /device:TPU:1, one launch (start us, length us, event | category | flops | bytes accessed | tf_op | source)
XLA Modules:
  0.0 161.1 jit_solution(12024472826073384881)
XLA Ops:
  0.0 1.4 copy.6.args_0_
  1.4 1.3 copy.7.args_1_
  2.7 154.9 %correlate.1 = f32[3,8,128,128]{3,2,1,0:T(8,128)} custom-call(s32[16,6]{1,0:T(8,128)} %copy.6.args_0_, s32[1,3,2]{2,1,0:T(4,128)} %copy.7.args_1_, bf16[2,2,2,128,1024]{4,3,2,1,0:T(8,128)(2,1)} %args_2_.4, f32[8,2,8,2,1024]{4,3,2,1,0:T(2,128)} %constant.4.clone.args_3_), custom_call_target="tpu_custom_call" | custom-call | tf_op jit(solution)/shard_map/correlate/pallas_call | solution.py:429
  158.3 2.8 %broadcast_select_fusion = f32[3,8,128,128]{3,2,1,0:T(8,128)} fusion(f32[3,8,128,128]{3,2,1,0:T(8,128)} %correlate.1, pred[3]{0:T(512)(128)(4,1)S(1)} %iota_compare_fusion), kind=kLoop, calls=%fused_computation | loop fusion | flops 393216 | bytes 3145731 | tf_op jit(solution)/shard_map/jit(_where)/select_n | solution.py:441
  (1 shorter events, 0.0 us)

commit v3 on v2

v3 whole, which is shorter than its diff:
```python
import math

import jax
import jax.numpy as jnp
import numpy as np
from jax import lax
from jax.experimental import pallas as pl
from jax.experimental.pallas import tpu as pltpu
from jax.sharding import PartitionSpec as P

MESH = pl.DeviceIdType.MESH
F = 8192
W = 2
LAGS = 64
CH = 128
BAND = 1024
NEED = 6
SLOTS = 3
SIDE = 4
T1 = 8
T0 = 8
WIDTHS = (256, 256, 256, 128, 128)
STARTS = (0, 256, 512, 768, 896)
CHUNKS = len(WIDTHS)
LAST = CHUNKS - 1
BUFFER = (0, 1, 0, 2, 3)
BUFFER_WIDTHS = (256, 256, 128, 128)
BUFFERS = len(BUFFER_WIDTHS)
EARLY = (0, 3, 3, 3, 2)
NORM = 1.0 / math.sqrt(2.0 * W * F)


COARSE = T0 * np.arange(T1) - LAGS // 2
FINE = -np.arange(T0)


def phase_tables():
    freqs = np.arange(BAND, dtype=np.int64)

    def table(shifts):
        angles = (freqs[None, :] * shifts[:, None] % F) * (2.0 * math.pi / F)
        return np.stack([np.cos(angles), np.sin(angles)], axis=1)

    base = np.stack([table(COARSE), table(FINE)]).astype(np.float32)
    bands = np.arange(F // BAND, dtype=np.int64)
    turns = (bands[:, None] * BAND * FINE[None, :] % F) * (2.0 * math.pi / F)
    turn = np.stack([np.cos(turns), np.sin(turns)], axis=-1).astype(np.float32)
    return base, np.repeat(turn[..., None], 128, axis=-1)


def pick(flags, values):
    total = jnp.int32(0)
    for flag, value in zip(flags, values, strict=True):
        total = total + jnp.where(flag, value, 0)
    return total


def request_plan(req_ref, node, along, across, by_y):
    rel, index = [], []
    for q in range(NEED):
        block = req_ref[q, node]
        holder = lax.div(block, 2)
        hy, hz = lax.div(holder, SIDE), lax.rem(holder, SIDE)
        h_along, h_across = (hy, hz) if by_y else (hz, hy)
        rel.append(lax.rem(h_along - along + SIDE, SIDE))
        index.append(2 * lax.rem(h_across - across + SIDE, SIDE) + lax.rem(block, 2))
    rank = []
    for q in range(NEED):
        total = jnp.int32(0)
        for earlier in range(q):
            total = total + jnp.where(rel[earlier] == rel[q], 1, 0)
        rank.append(total)
    n1 = pick([r == 1 for r in rel], [1] * NEED)
    n2 = pick([r == 2 for r in rel], [1] * NEED)
    plus = jnp.minimum(jnp.minimum(n2, 2), 4 - n1)
    return rel, index, rank, plus, n2 - plus


def kernel(*args):
    req_ref, pairs_ref, counts_hbm, x_hbm, tab_hbm, turn_hbm, o_ref = args[:7]
    rest = list(args[7:])

    def take(count):
        taken, rest[:count] = rest[:count], []
        return taken

    R = [take(CHUNKS) for _ in range(W)]
    FR = [take(CHUNKS) for _ in range(W)]
    TR = [take(CHUNKS) for _ in range(W)]
    FS = [take(BUFFERS) for _ in range(W)]
    TS = [take(BUFFERS) for _ in range(W)]
    tab, turn, u, v, acc, loc, counts_ref = take(7)
    PS, PR, S, XR, XS, YR = (take(SLOTS) for _ in range(6))
    local_sem, tab_sem, turn_sem, count_sem, s1, r1, s1b, r1b, st, rt, sf, rf, sp, rp, sx, rx = take(16)

    me, lag = lax.axis_index("tiles"), lax.axis_index("lag")
    y, z = lax.div(me, SIDE), lax.rem(me, SIDE)
    x, core = lax.div(lag, 2), lax.rem(lag, 2)

    def shift(a, by):
        return lax.rem(a + by + SIDE, SIDE)

    def at(by_y, by):
        return (shift(y, by) * SIDE + z, lag) if by_y else (y * SIDE + shift(z, by), lag)

    def along_x(by):
        return (me, shift(x, by) * 2 + core)

    partner = (me, 2 * x + 1 - core)

    tables = pltpu.make_async_copy(tab_hbm, tab, tab_sem)
    turns = pltpu.make_async_copy(turn_hbm.at[lag], turn, turn_sem)
    loads = {}
    for c in range(CHUNKS):
        for w in range(W):
            loads[c, w] = pltpu.make_async_copy(
                x_hbm.at[:, w, :, :, pl.ds(STARTS[c], WIDTHS[c])], R[w][c].at[0:2], local_sem.at[c, w]
            )
            loads[c, w].start()
    tables.start()
    turns.start()
    live_count = pltpu.make_async_copy(counts_hbm, counts_ref, count_sem)
    live_count.start()
    barrier = pltpu.get_barrier_semaphore()
    friends = [at(True, -1), at(True, 1), at(False, -1), at(False, 1)]
    friends += [along_x(-1), along_x(1), partner]
    for friend in friends:
        pl.semaphore_signal(barrier, inc=1, device_id=friend, device_id_type=MESH)
    pl.semaphore_wait(barrier, len(friends))

    def remote(src, dst, send, recv, to):
        copy = pltpu.make_async_remote_copy(
            src_ref=src, dst_ref=dst, send_sem=send, recv_sem=recv, device_id=to, device_id_type=MESH
        )
        copy.start()
        return copy

    first, second, transit, final, arrival = {}, {}, {}, {}, {}

    def start_first(c):
        for w in range(W):
            loads[c, w].wait()
            for k, (by, slot) in enumerate(((-1, 1), (1, 3))):
                for b in (k, 1 - k):
                    first[c, w, k, b] = remote(
                        R[w][c].at[b],
                        R[w][c].at[2 * slot + b],
                        s1.at[c, w, k, b],
                        r1.at[c, w, k, b],
                        at(w == 1, by),
                    )

    def start_second(c):
        for w in range(W):
            for k, (by, slot) in enumerate(((-1, 1), (1, 3))):
                first[c, w, k, k].wait_recv()
                second[c, w, k] = remote(
                    R[w][c].at[2 * slot + k],
                    R[w][c].at[4 + k],
                    s1b.at[c, w, k],
                    r1b.at[c, w, k],
                    at(w == 1, by),
                )

    start_first(0)
    start_first(1)

    finals, transits, passing = {}, {}, {}
    for w in range(W):
        along, across = (y, z) if w == 0 else (z, y)
        by_y = w == 0

        def plan(by):
            there = shift(along, by)
            node = there * SIDE + across if by_y else across * SIDE + there
            return request_plan(req_ref, node, there, across, by_y)

        for k, (by, mine) in enumerate(((-1, 1), (1, 3))):
            rel, index, rank, plus, minus = plan(by)
            for j in range(4):
                finals[w, k, j] = pick(
                    [(a == mine) & (b == j) for a, b in zip(rel, rank, strict=True)], index
                )
            passing[w, k] = (plus, minus)[k]
        rel, index, rank, plus, minus = plan(2)
        for j in range(2):
            transits[w, 0, j] = pick(
                [(a == 2) & (b < plus) & (b == j) for a, b in zip(rel, rank, strict=True)], index
            )
            transits[w, 1, j] = pick(
                [(a == 2) & (b - plus == j) for a, b in zip(rel, rank, strict=True)], index
            )
        rel, index, rank, plus, minus = plan(0)
        for q in range(NEED):
            r = rank[q]
            far = jnp.where(r < plus, 8 + 3 - r, 12 + 3 - (r - plus))
            where = jnp.where(rel[q] == 2, far, jnp.where(rel[q] == 3, 12 + r, 8 + r))
            loc[w, q] = jnp.where(rel[q] == 0, index[q], where)

    def start_third(c):
        if BUFFER[c] in BUFFER[:c]:
            before = BUFFER.index(BUFFER[c])
            for w in range(W):
                for k in range(2):
                    transit.pop((before, w, k)).wait_send()
                    final.pop((before, w, k, 0)).wait_send()
                    final.pop((before, w, k, 1)).wait_send()
        for w in range(W):
            for k in range(2):
                first[c, w, k, 1 - k].wait_recv()
                second[c, w, k].wait_recv()
        for w in range(W):
            for k in range(2):
                for j in range(2):
                    TS[w][BUFFER[c]][k, j] = R[w][c][transits[w, k, j]]
        for w in range(W):
            for k, by in enumerate((-1, 1)):
                transit[c, w, k] = remote(
                    TS[w][BUFFER[c]].at[k], TR[w][c].at[k], st.at[c, w, k], rt.at[c, w, k], at(w == 0, by)
                )
        for w in range(W):
            for k in range(2):
                for j in range(2):
                    FS[w][BUFFER[c]][k, j] = R[w][c][finals[w, k, j]]
        for w in range(W):
            for k, by in enumerate((-1, 1)):
                final[c, w, k, 0] = arrival[c, w, k, 0] = remote(
                    FS[w][BUFFER[c]].at[k, 0:2],
                    FR[w][c].at[4 * k : 4 * k + 2],
                    sf.at[c, w, k, 0],
                    rf.at[c, w, k, 0],
                    at(w == 0, by),
                )

    def start_fourth(c):
        for w in range(W):
            for k in range(2):
                transit[c, w, k].wait_recv()
        for w in range(W):
            for k in range(2):
                for j in (2, 3):
                    direct = R[w][c][finals[w, k, j]]
                    passed = TR[w][c][k, 3 - j]
                    FS[w][BUFFER[c]][k, j] = jnp.where(passing[w, k] > 3 - j, passed, direct)
        for w in range(W):
            for k, by in enumerate((-1, 1)):
                final[c, w, k, 1] = arrival[c, w, k, 1] = remote(
                    FS[w][BUFFER[c]].at[k, 2:4],
                    FR[w][c].at[4 * k + 2 : 4 * k + 4],
                    sf.at[c, w, k, 1],
                    rf.at[c, w, k, 1],
                    at(w == 0, by),
                )

    def wait_finals(c):
        for w in range(W):
            for k in range(2):
                arrival[c, w, k, 0].wait_recv()
                arrival[c, w, k, 1].wait_recv()

    def turn_fine():
        for t in range(T0):
            cos, sin = tab[1, t, 0:1, :], tab[1, t, 1:2, :]
            c, m = turn[t, 0:1, 0:1], turn[t, 1:2, 0:1]
            tab[1, t, 0:1, :] = cos * c - sin * m
            tab[1, t, 1:2, :] = cos * m + sin * c

    STRIP = 32

    def compute(c, s):
        kc, first_col = WIDTHS[c], STARTS[c]
        cols = slice(first_col, first_col + kc)
        for w in range(W):
            for side, dst in enumerate((u, v)):
                where = loc[w, pairs_ref[0, side, s]]
                i = lax.rem(where, 8)
                for r in range(0, CH, STRIP):
                    rows = slice(r, r + STRIP)
                    block = jnp.where(where < 8, R[w][c][i, :, rows, :], FR[w][c][i, :, rows, :])
                    real, imag = block[0].astype(jnp.float32), block[1].astype(jnp.float32)
                    base = 2 * w * kc
                    for t in range(8):
                        cos = tab[side, t, 0:1, cols]
                        sin = tab[side, t, 1:2, cols]
                        out = slice(t * CH + r, t * CH + r + STRIP)
                        dst[out, base : base + kc] = (real * cos - imag * sin).astype(jnp.bfloat16)
                        dst[out, base + kc : base + 2 * kc] = (real * sin + imag * cos).astype(
                            jnp.bfloat16
                        )
        part = lax.dot_general(
            u[:, : 4 * kc],
            v[:, : 4 * kc],
            (((1,), (1,)), ((), ())),
            preferred_element_type=jnp.float32,
        )
        if c == 0:
            acc[s] = part
        else:
            acc[s] += part

    def compute_some(c, slots):
        def one(s, carry):
            compute(c, s)
            return carry

        lax.fori_loop(0, slots, one, 0)

    pair_copy, x_copy = {}, {}
    ORDER = (2, 1, -1, 0)

    def rows_of(there, which):
        return pl.ds(pl.multiple_of((2 * there + which) * CH, CH), CH)

    def send_pair(s):
        for n, by in enumerate(ORDER):
            block = acc[s, rows_of(shift(x, by), 1 - core), :] * NORM
            PS[s][n] = block.astype(jnp.bfloat16)
            pair_copy[s, n] = remote(
                PS[s].at[n], PR[s].at[n], sp.at[s, n], rp.at[s, n], partner
            )

    HALF = T0 * CH // 2
    lo, hi = slice(0, HALF), slice(HALF, 2 * HALF)

    def chip_sum(s):
        def total(by):
            n = ORDER.index(by)
            pair_copy[s, n].wait_recv()
            mine = acc[s, rows_of(shift(x, by), core), :] * NORM
            return mine + PR[s][n].astype(jnp.float32)

        far = total(2).astype(jnp.bfloat16)
        XS[s][0, 0] = far[:, lo]
        XS[s][1, 0] = far[:, hi]
        for k, by in enumerate((1, -1)):
            x_copy[s, k, 0] = remote(
                XS[s].at[k, 0], XR[s].at[k, 0], sx.at[s, k, 0], rx.at[s, k, 0], along_x(by)
            )
        for k, by in enumerate((1, -1)):
            near = total(by)
            relayed, own = (lo, hi) if k == 0 else (hi, lo)
            YR[s][k] = near[:, relayed]
            XS[s][k, 1] = near[:, own].astype(jnp.bfloat16)
            x_copy[s, k, 1] = remote(
                XS[s].at[k, 1], XR[s].at[k, 1], sx.at[s, k, 1], rx.at[s, k, 1], along_x(by)
            )
        S[s][...] = total(0)

    def relay(s):
        for k, by in enumerate((1, -1)):
            x_copy[s, k, 0].wait_recv()
            XS[s][k, 2] = (YR[s][k] + XR[s][k, 0].astype(jnp.float32)).astype(jnp.bfloat16)
            x_copy[s, k, 2] = remote(
                XS[s].at[k, 2], XR[s].at[k, 2], sx.at[s, k, 2], rx.at[s, k, 2], along_x(by)
            )

    def finish(s):
        for k in range(2):
            x_copy[s, k, 1].wait_recv()
            x_copy[s, k, 2].wait_recv()
        low = S[s][:, lo] + XR[s][0, 2].astype(jnp.float32) + XR[s][1, 1].astype(jnp.float32)
        high = S[s][:, hi] + XR[s][0, 1].astype(jnp.float32) + XR[s][1, 2].astype(jnp.float32)
        live = s < counts_ref[0]
        for t in range(T0 // 2):
            o_ref[s, t] = jnp.where(live, low[:, t * CH : (t + 1) * CH], 0.0)
            o_ref[s, T0 // 2 + t] = jnp.where(live, high[:, t * CH : (t + 1) * CH], 0.0)

    tables.wait()
    turns.wait()
    turn_fine()
    live_count.wait()
    start_second(0)
    start_first(2)
    for c in range(CHUNKS):
        start_third(c)
        if c > 0:
            wait_finals(c - 1)
            compute_some(c - 1, EARLY[c])
        start_fourth(c)
        if c + 1 < CHUNKS:
            start_second(c + 1)
        if c + 3 < CHUNKS:
            start_first(c + 3)
        if c > 0:
            for n in range(EARLY[c], SLOTS):
                compute(c - 1, n)
    last = LAST
    wait_finals(last)
    compute(last, 0)
    send_pair(0)
    compute(last, 1)
    send_pair(1)
    chip_sum(0)
    compute(last, 2)
    send_pair(2)
    relay(0)
    chip_sum(1)
    relay(1)
    chip_sum(2)
    finish(0)
    relay(2)
    finish(1)
    finish(2)

    for copy in list(first.values()) + list(second.values()):
        copy.wait_send()
    for copy in list(transit.values()) + list(final.values()):
        copy.wait_send()
    for copy in list(pair_copy.values()) + list(x_copy.values()):
        copy.wait_send()


def per_device(spectra, requests, pairs, counts, tables, turns):
    bf16, f32 = jnp.bfloat16, jnp.float32
    vmem, dma = pltpu.VMEM, pltpu.SemaphoreType.DMA
    scratch = []
    for lead in ((8,), (8,), (2, 2)):
        scratch += [vmem((*lead, 2, CH, width), bf16) for width in WIDTHS] * W
    for lead in ((2, 4), (2, 2)):
        scratch += [vmem((*lead, 2, CH, width), bf16) for width in BUFFER_WIDTHS] * W
    scratch += [
        vmem((2, 8, 2, BAND), f32),
        vmem((8, 2, 128), f32),
        vmem((T1 * CH, 2 * W * max(WIDTHS)), bf16),
        vmem((T0 * CH, 2 * W * max(WIDTHS)), bf16),
        vmem((SLOTS, T1 * CH, T0 * CH), f32),
        pltpu.SMEM((W, NEED), jnp.int32),
        pltpu.SMEM((1,), jnp.int32),
    ]
    scratch += [vmem((SIDE, CH, T0 * CH), bf16)] * (2 * SLOTS)
    scratch += [vmem((CH, T0 * CH), f32)] * SLOTS
    scratch += [vmem((2, 3, CH, T0 * CH // 2), bf16)] * (2 * SLOTS)
    scratch += [vmem((2, CH, T0 * CH // 2), f32)] * SLOTS
    scratch += [
        dma((CHUNKS, W)),
        dma,
        dma,
        dma,
        dma((CHUNKS, W, 2, 2)),
        dma((CHUNKS, W, 2, 2)),
        dma((CHUNKS, W, 2)),
        dma((CHUNKS, W, 2)),
        dma((CHUNKS, W, 2)),
        dma((CHUNKS, W, 2)),
        dma((CHUNKS, W, 2, 2)),
        dma((CHUNKS, W, 2, 2)),
        dma((SLOTS, SIDE)),
        dma((SLOTS, SIDE)),
        dma((SLOTS, 2, 3)),
        dma((SLOTS, 2, 3)),
    ]
    smem = pl.BlockSpec(memory_space=pltpu.SMEM)
    hbm = pl.BlockSpec(memory_space=pl.ANY)
    return pl.pallas_call(
        kernel,
        out_shape=jax.ShapeDtypeStruct((SLOTS, T0, CH, CH), f32),
        in_specs=[smem, smem, hbm, hbm, hbm, hbm],
        out_specs=pl.BlockSpec(memory_space=pltpu.VMEM),
        scratch_shapes=scratch,
        compiler_params=pltpu.CompilerParams(
            collective_id=0, has_side_effects=True, vmem_limit_bytes=67043328
        ),
        name="correlate",
    )(requests.T, pairs.transpose(0, 2, 1), counts, spectra, tables, turns)


def solution(mesh):
    placed = (P("tiles", None, None, None, "lag"), P(), P("tiles", None, None), P("tiles"), P(), P())
    tables, turns = phase_tables()
    mapped = jax.shard_map(
        per_device,
        mesh=mesh,
        in_specs=placed,
        out_specs=P("tiles", "lag", None, None),
        check_vma=False,
    )

    def run(spectra, requests, pairs, counts):
        return mapped(spectra, requests, pairs, counts, jnp.asarray(tables), jnp.asarray(turns))

    return run
```

time: 161 us -> 154 us (0.957)
  Pallas kernels: 155 us -> 151 us
  other arithmetic: 2.8 us -> 0 us
    pallas_call x1, Pallas kernels: 155 us -> 151 us  [per_device(): pl.pallas_call(kernel, out_shape=jax.ShapeDtypeStruct((SLOTS, T0, CH, CH)...]
    select_n x1 -> x0, other arithmetic: 2.8 us -> none  [per_device(): return jnp.where(live[:, None, None, None], summed, 0.0)]
where the time goes in v3:
time: 154 us
  Pallas kernels  151 us (98%)
  local copies, waits for them, and re-layouts  2.7 us (2%)
    pallas_call x1, Pallas kernels, per_device(): pl.pallas_call(kernel, out_shape=jax.ShapeDtypeStruct((SLOTS, T0, CH, CH)...  151 us

profile of v3, /device:TPU:1, one launch (start us, length us, event | category | flops | bytes accessed | tf_op | source)
XLA Modules:
  0.0 154.1 jit_solution(4131195262393446671)
XLA Ops:
  0.7 150.8 %correlate.1 = f32[3,8,128,128]{3,2,1,0:T(8,128)} custom-call(s32[6,16]{1,0:T(8,128)} %bitcast.2, s32[1,2,3]{2,1,0:T(2,128)} %bitcast.3, s32[1]{0:T(128)S(6)} %copy.8.args_2_, bf16[2,2,2,128,1024]{4,3,2,1,0:T(8,128)(2,1)} %args_3_.4, f32[2,8,2,1024]{3,2,1,0:T(2,128)} %constant.4.clone.args_4_, f32[8,8,2,128]{3,2,1,0:T(2,128)} %constant.5.clone.args_5_), custom_call_target="tpu_custom_call" | custom-call | tf_op jit(solution)/shard_map/correlate/pallas_call | solution.py:454
  151.4 2.7 %copy.9 = f32[3,8,128,128]{3,2,1,0:T(8,128)} copy(f32[3,8,128,128]{3,2,1,0:T(8,128)} %correlate.1) | data formatting | bytes 3145728

commit v4 on v3

--- a/solution.py
+++ b/solution.py
@@ -1,3 +1,4 @@
+import functools
 import math
 
 import jax
@@ -26,6 +27,7 @@
 BUFFER = (0, 1, 0, 2, 3)
 BUFFER_WIDTHS = (256, 256, 128, 128)
 BUFFERS = len(BUFFER_WIDTHS)
+ENTRIES = {True: 5, False: 6}
 EARLY = (0, 3, 3, 3, 2)
 NORM = 1.0 / math.sqrt(2.0 * W * F)
 
@@ -55,43 +57,95 @@
     return total
 
 
-def request_plan(req_ref, node, along, across, by_y):
+def where_lies(req_ref, node, q, along, by_y):
+    block = req_ref[q, node]
+    holder = lax.div(block, 2)
+    hy, hz = lax.div(holder, SIDE), lax.rem(holder, SIDE)
+    h_along, h_across = (hy, hz) if by_y else (hz, hy)
+    return lax.rem(h_along - along + SIDE, SIDE), h_across, lax.rem(block, 2)
+
+
+def node_of(along, across, by_y):
+    return along * SIDE + across if by_y else across * SIDE + along
+
+
+def request_plan(req_ref, along, across, by_y):
     rel, index = [], []
     for q in range(NEED):
-        block = req_ref[q, node]
-        holder = lax.div(block, 2)
-        hy, hz = lax.div(holder, SIDE), lax.rem(holder, SIDE)
-        h_along, h_across = (hy, hz) if by_y else (hz, hy)
-        rel.append(lax.rem(h_along - along + SIDE, SIDE))
-        index.append(2 * lax.rem(h_across - across + SIDE, SIDE) + lax.rem(block, 2))
+        r, h_across, inside = where_lies(
+            req_ref, node_of(along, across, by_y), q, along, by_y
+        )
+        rel.append(r)
+        index.append(2 * lax.rem(h_across - across + SIDE, SIDE) + inside)
     rank = []
     for q in range(NEED):
         total = jnp.int32(0)
         for earlier in range(q):
             total = total + jnp.where(rel[earlier] == rel[q], 1, 0)
         rank.append(total)
-    n1 = pick([r == 1 for r in rel], [1] * NEED)
-    n2 = pick([r == 2 for r in rel], [1] * NEED)
-    plus = jnp.minimum(jnp.minimum(n2, 2), 4 - n1)
-    return rel, index, rank, plus, n2 - plus
-
-
-def kernel(*args):
+    return rel, index, rank
+
+
+def ring_plan(req_ref, across, by_y, tight):
+    near, far, below = [], [], []
+    for i in range(SIDE):
+        rel = [
+            where_lies(req_ref, node_of(i, across, by_y), q, i, by_y)[0] for q in range(NEED)
+        ]
+        for into, value in ((near, 1), (far, 2), (below, 3)):
+            into.append(pick([r == value for r in rel], [1] * NEED))
+    if not tight:
+        plus = [jnp.minimum(jnp.minimum(f, 2), 4 - n) for n, f in zip(near, far, strict=True)]
+        return near, far, below, plus, None
+
+    def clamp(value, f):
+        return jnp.minimum(jnp.maximum(value, jnp.maximum(f - 2, 0)), jnp.minimum(f, 2))
+
+    def half(value):
+        return lax.div(value + 16, 2) - 8
+
+    def attempt(up, order):
+        p = [clamp(half(below[i] - near[i] + far[i] + 1 - up), far[i]) for i in range(SIDE)]
+        for i in order:
+            j, k = (i + 1) % SIDE, (i - 1) % SIDE
+            high = jnp.maximum(near[i] + p[k], near[j] + p[j])
+            low = jnp.maximum(below[i] + far[j] - p[j], below[k] + far[k] - p[k])
+            p[i] = clamp(half(low + far[i] - high + up), far[i])
+        good = jnp.int32(1)
+        for i in range(SIDE):
+            j, k = (i + 1) % SIDE, (i - 1) % SIDE
+            for final, passing in (
+                (near[i] + p[i], p[k]),
+                (below[i] + far[i] - p[i], far[j] - p[j]),
+            ):
+                fits = (final <= 3) & (passing <= 2) | (final == 4) & (passing <= 1)
+                good = good * jnp.where(fits, 1, 0)
+            good = good * jnp.where(far[i] - p[i] <= 2, 1, 0) * jnp.where(p[i] <= 2, 1, 0)
+        return p, good
+
+    first, good = attempt(1, (0, 1, 2, 3))
+    second, also = attempt(0, (3, 2, 1, 0))
+    plus = [jnp.where(good == 1, a, b) for a, b in zip(first, second, strict=True)]
+    return near, far, below, plus, jnp.maximum(good, also)
+
+
+def kernel(tight, *args):
     req_ref, pairs_ref, counts_hbm, x_hbm, tab_hbm, turn_hbm, o_ref = args[:7]
-    rest = list(args[7:])
+    fits_ref = args[7] if tight else None
+    rest = list(args[8:] if tight else args[7:])
+    entries = ENTRIES[tight]
+    first_finals = slice(2, entries - 2), slice(entries - 2, entries)
 
     def take(count):
         taken, rest[:count] = rest[:count], []
         return taken
 
     R = [take(CHUNKS) for _ in range(W)]
-    FR = [take(CHUNKS) for _ in range(W)]
-    TR = [take(CHUNKS) for _ in range(W)]
-    FS = [take(BUFFERS) for _ in range(W)]
-    TS = [take(BUFFERS) for _ in range(W)]
+    G = [take(CHUNKS) for _ in range(W)]
+    GS = [take(BUFFERS) for _ in range(W)]
     tab, turn, u, v, acc, loc, counts_ref = take(7)
     PS, PR, S, XR, XS, YR = (take(SLOTS) for _ in range(6))
-    local_sem, tab_sem, turn_sem, count_sem, s1, r1, s1b, r1b, st, rt, sf, rf, sp, rp, sx, rx = take(16)
+    local_sem, tab_sem, turn_sem, count_sem, s1, r1, s1b, r1b, sg, rg, sp, rp, sx, rx = take(14)
 
     me, lag = lax.axis_index("tiles"), lax.axis_index("lag")
     y, z = lax.div(me, SIDE), lax.rem(me, SIDE)
@@ -165,37 +219,68 @@
     start_first(0)
     start_first(1)
 
-    finals, transits, passing = {}, {}, {}
+    direct, passed_on, shared, coming = {}, {}, {}, {}
     for w in range(W):
         along, across = (y, z) if w == 0 else (z, y)
         by_y = w == 0
-
-        def plan(by):
+        near, far, below, plus, _ = ring_plan(req_ref, across, by_y, tight)
+
+        def of(values, there):
+            return pick([there == i for i in range(SIDE)], values)
+
+        for k, (by, mine, count) in enumerate(((-1, 1, near), (1, 3, below))):
             there = shift(along, by)
-            node = there * SIDE + across if by_y else across * SIDE + there
-            return request_plan(req_ref, node, there, across, by_y)
-
-        for k, (by, mine) in enumerate(((-1, 1), (1, 3))):
-            rel, index, rank, plus, minus = plan(by)
+            rel, index, rank = request_plan(req_ref, there, across, by_y)
             for j in range(4):
-                finals[w, k, j] = pick(
+                direct[w, k, j] = pick(
                     [(a == mine) & (b == j) for a, b in zip(rel, rank, strict=True)], index
                 )
-            passing[w, k] = (plus, minus)[k]
-        rel, index, rank, plus, minus = plan(2)
+            up = of(plus, there)
+            coming[w, k] = up if k == 0 else of(far, there) - up
+            shared[w, k] = of(count, there) + coming[w, k] == 4
+        there = shift(along, 2)
+        rel, index, rank = request_plan(req_ref, there, across, by_y)
+        up = of(plus, there)
         for j in range(2):
-            transits[w, 0, j] = pick(
-                [(a == 2) & (b < plus) & (b == j) for a, b in zip(rel, rank, strict=True)], index
-            )
-            transits[w, 1, j] = pick(
-                [(a == 2) & (b - plus == j) for a, b in zip(rel, rank, strict=True)], index
-            )
-        rel, index, rank, plus, minus = plan(0)
+            passed_on[w, 0, j] = pick(
+                [(a == 2) & (b < up) & (b == j) for a, b in zip(rel, rank, strict=True)], index
+            )
+            passed_on[w, 1, j] = pick(
+                [(a == 2) & (b - up == j) for a, b in zip(rel, rank, strict=True)], index
+            )
+        if tight:
+            for k in range(2):
+                n = coming[w, k]
+                last_direct = jnp.where(
+                    n == 0, direct[w, k, 3], jnp.where(n == 1, direct[w, k, 2], direct[w, k, 1])
+                )
+                passed_on[w, k, 1] = jnp.where(shared[w, k], last_direct, passed_on[w, k, 1])
+        rel, index, rank = request_plan(req_ref, along, across, by_y)
+        up = of(plus, along)
         for q in range(NEED):
             r = rank[q]
-            far = jnp.where(r < plus, 8 + 3 - r, 12 + 3 - (r - plus))
-            where = jnp.where(rel[q] == 2, far, jnp.where(rel[q] == 3, 12 + r, 8 + r))
-            loc[w, q] = jnp.where(rel[q] == 0, index[q], where)
+            entry = []
+            for k, (count, n) in enumerate(((near, up), (below, of(far, along) - up))):
+                total = of(count, along)
+                e = 2 + r
+                if tight:
+                    e = jnp.where((total + n == 4) & (r == total - 1), 1, e)
+                entry.append(8 + k * entries + e)
+            two = jnp.where(
+                r < up, 8 + entries - 1 - r, 8 + 2 * entries - 1 - (r - up)
+            )
+            found = jnp.where(rel[q] == 2, two, jnp.where(rel[q] == 3, entry[1], entry[0]))
+            loc[w, q] = jnp.where(rel[q] == 0, index[q], found)
+    if tight:
+        good = jnp.int32(1)
+        for w in range(W):
+            good = lax.fori_loop(
+                0,
+                SIDE,
+                lambda across, so_far, w=w: so_far * ring_plan(req_ref, across, w == 0, True)[4],
+                good,
+            )
+        fits_ref[0] = good
 
     def start_third(c):
         if BUFFER[c] in BUFFER[:c]:
@@ -212,25 +297,28 @@
         for w in range(W):
             for k in range(2):
                 for j in range(2):
-                    TS[w][BUFFER[c]][k, j] = R[w][c][transits[w, k, j]]
-        for w in range(W):
-            for k, by in enumerate((-1, 1)):
-                transit[c, w, k] = remote(
-                    TS[w][BUFFER[c]].at[k], TR[w][c].at[k], st.at[c, w, k], rt.at[c, w, k], at(w == 0, by)
-                )
-        for w in range(W):
-            for k in range(2):
-                for j in range(2):
-                    FS[w][BUFFER[c]][k, j] = R[w][c][finals[w, k, j]]
-        for w in range(W):
-            for k, by in enumerate((-1, 1)):
-                final[c, w, k, 0] = arrival[c, w, k, 0] = remote(
-                    FS[w][BUFFER[c]].at[k, 0:2],
-                    FR[w][c].at[4 * k : 4 * k + 2],
-                    sf.at[c, w, k, 0],
-                    rf.at[c, w, k, 0],
-                    at(w == 0, by),
-                )
+                    GS[w][BUFFER[c]][k * entries + j] = R[w][c][passed_on[w, k, j]]
+        for w in range(W):
+            for k in range(2):
+                transit[c, w, k] = send_group(c, w, k, 0, slice(0, 2))
+        for w in range(W):
+            for k in range(2):
+                for j in range(entries - 4):
+                    GS[w][BUFFER[c]][k * entries + 2 + j] = R[w][c][direct[w, k, j]]
+        for w in range(W):
+            for k in range(2):
+                final[c, w, k, 0] = send_group(c, w, k, 1, first_finals[0])
+                arrival[c, w, k, 0] = final[c, w, k, 0]
+
+    def send_group(c, w, k, group, which):
+        rows = slice(k * entries + which.start, k * entries + which.stop)
+        return remote(
+            GS[w][BUFFER[c]].at[rows],
+            G[w][c].at[rows],
+            sg.at[c, w, k, group],
+            rg.at[c, w, k, group],
+            at(w == 0, (-1, 1)[k]),
+        )
 
     def start_fourth(c):
         for w in range(W):
@@ -238,19 +326,17 @@
                 transit[c, w, k].wait_recv()
         for w in range(W):
             for k in range(2):
-                for j in (2, 3):
-                    direct = R[w][c][finals[w, k, j]]
-                    passed = TR[w][c][k, 3 - j]
-                    FS[w][BUFFER[c]][k, j] = jnp.where(passing[w, k] > 3 - j, passed, direct)
-        for w in range(W):
-            for k, by in enumerate((-1, 1)):
-                final[c, w, k, 1] = arrival[c, w, k, 1] = remote(
-                    FS[w][BUFFER[c]].at[k, 2:4],
-                    FR[w][c].at[4 * k + 2 : 4 * k + 4],
-                    sf.at[c, w, k, 1],
-                    rf.at[c, w, k, 1],
-                    at(w == 0, by),
-                )
+                for n in (1, 0):
+                    e = entries - 1 - n
+                    own = R[w][c][direct[w, k, e - 2]]
+                    passing = G[w][c][k * entries + n]
+                    GS[w][BUFFER[c]][k * entries + e] = jnp.where(
+                        coming[w, k] > n, passing, own
+                    )
+        for w in range(W):
+            for k in range(2):
+                final[c, w, k, 1] = send_group(c, w, k, 2, first_finals[1])
+                arrival[c, w, k, 1] = final[c, w, k, 1]
 
     def wait_finals(c):
         for w in range(W):
@@ -273,37 +359,59 @@
         for w in range(W):
             for side, dst in enumerate((u, v)):
                 where = loc[w, pairs_ref[0, side, s]]
-                i = lax.rem(where, 8)
-                for r in range(0, CH, STRIP):
-                    rows = slice(r, r + STRIP)
-                    block = jnp.where(where < 8, R[w][c][i, :, rows, :], FR[w][c][i, :, rows, :])
+                i = jnp.minimum(where, 7)
+                g = jnp.minimum(jnp.maximum(where - 8, 0), 2 * entries - 1)
+
+                def strip(r, carry, w=w, side=side, dst=dst, i=i, g=g, where=where):
+                    rows = pl.ds(pl.multiple_of(r * STRIP, STRIP), STRIP)
+                    block = jnp.where(
+                        where < 8, R[w][c][i, :, rows, :], G[w][c][g, :, rows, :]
+                    )
                     real, imag = block[0].astype(jnp.float32), block[1].astype(jnp.float32)
                     base = 2 * w * kc
                     for t in range(8):
                         cos = tab[side, t, 0:1, cols]
                         sin = tab[side, t, 1:2, cols]
-                        out = slice(t * CH + r, t * CH + r + STRIP)
+                        out = pl.ds(pl.multiple_of(t * CH + r * STRIP, STRIP), STRIP)
                         dst[out, base : base + kc] = (real * cos - imag * sin).astype(jnp.bfloat16)
                         dst[out, base + kc : base + 2 * kc] = (real * sin + imag * cos).astype(
                             jnp.bfloat16
                         )
-        part = lax.dot_general(
-            u[:, : 4 * kc],
-            v[:, : 4 * kc],
-            (((1,), (1,)), ((), ())),
-            preferred_element_type=jnp.float32,
-        )
-        if c == 0:
-            acc[s] = part
+                    return carry
+
+                if tight:
+                    for r in range(CH // STRIP):
+                        strip(r, 0)
+                else:
+                    lax.fori_loop(0, CH // STRIP, strip, 0)
+
+        wide = T0 * CH if tight else 256
+
+        def multiply(n, carry):
+            span = pl.ds(pl.multiple_of(n * wide, wide), wide)
+            part = lax.dot_general(
+                u[:, : 4 * kc],
+                v[span, : 4 * kc],
+                (((1,), (1,)), ((), ())),
+                preferred_element_type=jnp.float32,
+            )
+            if c == 0:
+                acc[s, :, span] = part
+            else:
+                acc[s, :, span] += part
+            return carry
+
+        if tight:
+            multiply(0, 0)
         else:
-            acc[s] += part
-
-    def compute_some(c, slots):
+            lax.fori_loop(0, T0 * CH // wide, multiply, 0)
+
+    def compute_some(c, slots, begin=0):
         def one(s, carry):
             compute(c, s)
             return carry
 
-        lax.fori_loop(0, slots, one, 0)
+        lax.fori_loop(begin, slots, one, 0)
 
     pair_copy, x_copy = {}, {}
     ORDER = (2, 1, -1, 0)
@@ -410,14 +518,14 @@
         copy.wait_send()
 
 
-def per_device(spectra, requests, pairs, counts, tables, turns):
+def correlate(tight, spectra, requests, pairs, counts, tables, turns):
+    entries = ENTRIES[tight]
     bf16, f32 = jnp.bfloat16, jnp.float32
     vmem, dma = pltpu.VMEM, pltpu.SemaphoreType.DMA
     scratch = []
-    for lead in ((8,), (8,), (2, 2)):
-        scratch += [vmem((*lead, 2, CH, width), bf16) for width in WIDTHS] * W
-    for lead in ((2, 4), (2, 2)):
-        scratch += [vmem((*lead, 2, CH, width), bf16) for width in BUFFER_WIDTHS] * W
+    for lead in (8, 2 * entries):
+        scratch += [vmem((lead, 2, CH, width), bf16) for width in WIDTHS] * W
+    scratch += [vmem((2 * entries, 2, CH, width), bf16) for width in BUFFER_WIDTHS] * W
     scratch += [
         vmem((2, 8, 2, BAND), f32),
         vmem((8, 2, 128), f32),
@@ -440,10 +548,8 @@
         dma((CHUNKS, W, 2, 2)),
         dma((CHUNKS, W, 2)),
         dma((CHUNKS, W, 2)),
-        dma((CHUNKS, W, 2)),
-        dma((CHUNKS, W, 2)),
-        dma((CHUNKS, W, 2, 2)),
-        dma((CHUNKS, W, 2, 2)),
+        dma((CHUNKS, W, 2, 3)),
+        dma((CHUNKS, W, 2, 3)),
         dma((SLOTS, SIDE)),
         dma((SLOTS, SIDE)),
         dma((SLOTS, 2, 3)),
@@ -451,17 +557,27 @@
     ]
     smem = pl.BlockSpec(memory_space=pltpu.SMEM)
     hbm = pl.BlockSpec(memory_space=pl.ANY)
+    out_shape = [jax.ShapeDtypeStruct((SLOTS, T0, CH, CH), f32)]
+    out_specs = [pl.BlockSpec(memory_space=pltpu.VMEM)]
+    if tight:
+        out_shape.append(jax.ShapeDtypeStruct((1,), jnp.int32))
+        out_specs.append(smem)
     return pl.pallas_call(
-        kernel,
-        out_shape=jax.ShapeDtypeStruct((SLOTS, T0, CH, CH), f32),
+        functools.partial(kernel, tight),
+        out_shape=out_shape,
         in_specs=[smem, smem, hbm, hbm, hbm, hbm],
-        out_specs=pl.BlockSpec(memory_space=pltpu.VMEM),
+        out_specs=out_specs,
         scratch_shapes=scratch,
         compiler_params=pltpu.CompilerParams(
-            collective_id=0, has_side_effects=True, vmem_limit_bytes=67043328
+            collective_id=0 if tight else 1, has_side_effects=True, vmem_limit_bytes=67043328
         ),
-        name="correlate",
+        name="correlate_tight" if tight else "correlate_any",
     )(requests.T, pairs.transpose(0, 2, 1), counts, spectra, tables, turns)
+
+
+def per_device(*operands):
+    summed, fits = correlate(True, *operands)
+    return lax.cond(fits[0] == 1, lambda: summed, lambda: correlate(False, *operands)[0])
 
 
 def solution(mesh):

time: 154 us -> 147 us (0.955)
  Pallas kernels: 151 us -> 143 us
    pallas_call x1, Pallas kernels: 151 us -> 143 us  [correlate(): pl.pallas_call(functools.partial(kernel, tight), out_shape=out_shape, in_...]
where the time goes in v4:
time: 147 us
  Pallas kernels  143 us (97%)
  local copies, waits for them, and re-layouts  2.7 us (2%)
    pallas_call x1, Pallas kernels, correlate(): pl.pallas_call(functools.partial(kernel, tight), out_shape=out_shape, in_...  143 us

profile of v4, /device:TPU:1, one launch (start us, length us, event | category | flops | bytes accessed | tf_op | source)
XLA Modules:
  0.0 146.8 jit_solution(5743035167175966314)
XLA Ops:
  0.7 142.8 %correlate_tight.1 = (f32[3,8,128,128]{3,2,1,0:T(8,128)}, s32[1]{0:T(128)}) custom-call(s32[6,16]{1,0:T(8,128)} %bitcast.5, s32[1,2,3]{2,1,0:T(2,128)} %bitcast.7, s32[1]{0:T(128)S(6)} %copy.12.args_2_, bf16[2,2,2,128,1024]{4,3,2,1,0:T(8,128)(2,1)} %args_3_.4, f32[2,8,2,1024]{3,2,1,0:T(2,128)} %constant.7.clone.args_4_, f32[8,8,2,128]{3,2,1,0:T(2,128)} %constant.8.clone.args_5_), custom_call_target="tpu_custom_call" | custom-call | tf_op jit(solution)/shard_map/correlate_tight/pallas_call | solution.py:565
  144.1 2.7 %copy.13 = f32[3,8,128,128]{3,2,1,0:T(8,128)} copy(f32[3,8,128,128]{3,2,1,0:T(8,128)} %get-tuple-element.31) | data formatting | bytes 3145728
  (1 shorter events, 0.0 us)

commit v5 on v4

--- a/solution.py
+++ b/solution.py
@@ -20,15 +20,16 @@
 SIDE = 4
 T1 = 8
 T0 = 8
-WIDTHS = (256, 256, 256, 128, 128)
-STARTS = (0, 256, 512, 768, 896)
+WIDTHS = (256, 256, 256, 256)
+STARTS = (0, 256, 512, 768)
 CHUNKS = len(WIDTHS)
 LAST = CHUNKS - 1
-BUFFER = (0, 1, 0, 2, 3)
-BUFFER_WIDTHS = (256, 256, 128, 128)
+BUFFER = (0, 1, 0, 1)
+BUFFER_WIDTHS = (256, 256)
 BUFFERS = len(BUFFER_WIDTHS)
 ENTRIES = {True: 5, False: 6}
-EARLY = (0, 3, 3, 3, 2)
+BEFORE_FOURTH = ((), ((0, 0, 3),), ((1, 0, 3),), ((2, 0, 2),))
+AFTER_FOURTH = ((), (), (), ((2, 2, 3),))
 NORM = 1.0 / math.sqrt(2.0 * W * F)
 
 
@@ -406,12 +407,18 @@
         else:
             lax.fori_loop(0, T0 * CH // wide, multiply, 0)
 
-    def compute_some(c, slots, begin=0):
+    def compute_some(c, begin, end):
+        if begin == 0:
+            wait_finals(c)
+        if end - begin == 1:
+            compute(c, begin)
+            return
+
         def one(s, carry):
             compute(c, s)
             return carry
 
-        lax.fori_loop(begin, slots, one, 0)
+        lax.fori_loop(begin, end, one, 0)
 
     pair_copy, x_copy = {}, {}
     ORDER = (2, 1, -1, 0)
@@ -470,8 +477,9 @@
         high = S[s][:, hi] + XR[s][0, 1].astype(jnp.float32) + XR[s][1, 2].astype(jnp.float32)
         live = s < counts_ref[0]
         for t in range(T0 // 2):
-            o_ref[s, t] = jnp.where(live, low[:, t * CH : (t + 1) * CH], 0.0)
-            o_ref[s, T0 // 2 + t] = jnp.where(live, high[:, t * CH : (t + 1) * CH], 0.0)
+            span = slice(t * CH, (t + 1) * CH)
+            o_ref[s, t] = jnp.where(live, low[:, span], 0.0).astype(jnp.bfloat16)
+            o_ref[s, T0 // 2 + t] = jnp.where(live, high[:, span], 0.0).astype(jnp.bfloat16)
 
     tables.wait()
     turns.wait()
@@ -481,30 +489,28 @@
     start_first(2)
     for c in range(CHUNKS):
         start_third(c)
-        if c > 0:
-            wait_finals(c - 1)
-            compute_some(c - 1, EARLY[c])
-        start_fourth(c)
         if c + 1 < CHUNKS:
             start_second(c + 1)
         if c + 3 < CHUNKS:
             start_first(c + 3)
-        if c > 0:
-            for n in range(EARLY[c], SLOTS):
-                compute(c - 1, n)
+        for chunk, begin, end in BEFORE_FOURTH[c]:
+            compute_some(chunk, begin, end)
+        start_fourth(c)
+        for chunk, begin, end in AFTER_FOURTH[c]:
+            compute_some(chunk, begin, end)
     last = LAST
     wait_finals(last)
     compute(last, 0)
     send_pair(0)
+    chip_sum(0)
     compute(last, 1)
     send_pair(1)
-    chip_sum(0)
     compute(last, 2)
     send_pair(2)
     relay(0)
     chip_sum(1)
+    chip_sum(2)
     relay(1)
-    chip_sum(2)
     finish(0)
     relay(2)
     finish(1)
@@ -557,7 +563,7 @@
     ]
     smem = pl.BlockSpec(memory_space=pltpu.SMEM)
     hbm = pl.BlockSpec(memory_space=pl.ANY)
-    out_shape = [jax.ShapeDtypeStruct((SLOTS, T0, CH, CH), f32)]
+    out_shape = [jax.ShapeDtypeStruct((SLOTS, T0, CH, CH), bf16)]
     out_specs = [pl.BlockSpec(memory_space=pltpu.VMEM)]
     if tight:
         out_shape.append(jax.ShapeDtypeStruct((1,), jnp.int32))
@@ -577,7 +583,8 @@
 
 def per_device(*operands):
     summed, fits = correlate(True, *operands)
-    return lax.cond(fits[0] == 1, lambda: summed, lambda: correlate(False, *operands)[0])
+    chosen = lax.cond(fits[0] == 1, lambda: summed, lambda: correlate(False, *operands)[0])
+    return chosen.astype(jnp.float32)
 
 
 def solution(mesh):

time: 147 us -> 139 us (0.946)
  Pallas kernels: 143 us -> 135 us
  local copies, waits for them, and re-layouts: 2.7 us -> 0 us
  other arithmetic: 0 us -> 2.45 us
    pallas_call x1, Pallas kernels: 143 us -> 135 us  [correlate(): pl.pallas_call(functools.partial(kernel, tight), out_shape=out_shape, in_...]
    unnamed x1 -> x0, local copies, waits for them, and re-layouts: 2.7 us -> none
    convert_element_type x0 -> x1, other arithmetic: none -> 2.45 us  [per_device(): return chosen.astype(jnp.float32)]
where the time goes in v5:
time: 139 us
  Pallas kernels  135 us (97%)
  other arithmetic  2.45 us (2%)
    pallas_call x1, Pallas kernels, correlate(): pl.pallas_call(functools.partial(kernel, tight), out_shape=out_shape, in_...  135 us

profile of v5, /device:TPU:1, one launch (start us, length us, event | category | flops | bytes accessed | tf_op | source)
XLA Modules:
  0.0 139.1 jit_solution(15936344811816384081)
XLA Ops:
  0.7 135.3 %correlate_tight.1 = (bf16[3,8,128,128]{3,2,1,0:T(8,128)(2,1)}, s32[1]{0:T(128)}) custom-call(s32[6,16]{1,0:T(8,128)} %bitcast.5, s32[1,2,3]{2,1,0:T(2,128)} %bitcast.7, s32[1]{0:T(128)S(6)} %copy.9.args_2_, bf16[2,2,2,128,1024]{4,3,2,1,0:T(8,128)(2,1)} %args_3_.4, f32[2,8,2,1024]{3,2,1,0:T(2,128)} %constant.7.clone.args_4_, ...), custom_call_target="tpu_custom_call" | custom-call | tf_op jit(solution)/shard_map/correlate_tight/pallas_call | solution.py:571
  136.6 2.5 %convert_element_type.17 = f32[3,8,128,128]{3,2,1,0:T(8,128)} convert(bf16[3,8,128,128]{3,2,1,0:T(8,128)(2,1)} %get-tuple-element.39) | non-fusion elementwise | flops 393216 | bytes 2359296 | tf_op jit(solution)/shard_map/convert_element_type | solution.py:587
  (1 shorter events, 0.0 us)

commit v6 on v5

--- a/solution.py
+++ b/solution.py
@@ -163,6 +163,11 @@
 
     partner = (me, 2 * x + 1 - core)
 
+    barrier = pltpu.get_barrier_semaphore()
+    friends = [at(True, -1), at(True, 1), at(False, -1), at(False, 1)]
+    friends += [along_x(-1), along_x(1), partner]
+    for friend in friends:
+        pl.semaphore_signal(barrier, inc=1, device_id=friend, device_id_type=MESH)
     tables = pltpu.make_async_copy(tab_hbm, tab, tab_sem)
     turns = pltpu.make_async_copy(turn_hbm.at[lag], turn, turn_sem)
     loads = {}
@@ -176,11 +181,6 @@
     turns.start()
     live_count = pltpu.make_async_copy(counts_hbm, counts_ref, count_sem)
     live_count.start()
-    barrier = pltpu.get_barrier_semaphore()
-    friends = [at(True, -1), at(True, 1), at(False, -1), at(False, 1)]
-    friends += [along_x(-1), along_x(1), partner]
-    for friend in friends:
-        pl.semaphore_signal(barrier, inc=1, device_id=friend, device_id_type=MESH)
     pl.semaphore_wait(barrier, len(friends))
 
     def remote(src, dst, send, recv, to):
@@ -371,9 +371,13 @@
                     real, imag = block[0].astype(jnp.float32), block[1].astype(jnp.float32)
                     base = 2 * w * kc
                     for t in range(8):
+                        out = pl.ds(pl.multiple_of(t * CH + r * STRIP, STRIP), STRIP)
+                        if (COARSE, FINE)[side][t] == 0:
+                            dst[out, base : base + kc] = block[0]
+                            dst[out, base + kc : base + 2 * kc] = block[1]
+                            continue
                         cos = tab[side, t, 0:1, cols]
                         sin = tab[side, t, 1:2, cols]
-                        out = pl.ds(pl.multiple_of(t * CH + r * STRIP, STRIP), STRIP)
                         dst[out, base : base + kc] = (real * cos - imag * sin).astype(jnp.bfloat16)
                         dst[out, base + kc : base + 2 * kc] = (real * sin + imag * cos).astype(
                             jnp.bfloat16

time: 139 us -> 139 us (level)
  no operation moved by 1% of the time
where the time goes in v6:
time: 139 us
  Pallas kernels  135 us (97%)
  other arithmetic  2.45 us (2%)
    pallas_call x1, Pallas kernels, correlate(): pl.pallas_call(functools.partial(kernel, tight), out_shape=out_shape, in_...  135 us

profile of v6, /device:TPU:1, one launch (start us, length us, event | category | flops | bytes accessed | tf_op | source)
XLA Modules:
  0.0 139.1 jit_solution(1529966182906099471)
XLA Ops:
  0.7 135.3 %correlate_tight.1 = (bf16[3,8,128,128]{3,2,1,0:T(8,128)(2,1)}, s32[1]{0:T(128)}) custom-call(s32[6,16]{1,0:T(8,128)} %bitcast.5, s32[1,2,3]{2,1,0:T(2,128)} %bitcast.7, s32[1]{0:T(128)S(6)} %copy.9.args_2_, bf16[2,2,2,128,1024]{4,3,2,1,0:T(8,128)(2,1)} %args_3_.4, f32[2,8,2,1024]{3,2,1,0:T(2,128)} %constant.7.clone.args_4_, ...), custom_call_target="tpu_custom_call" | custom-call | tf_op jit(solution)/shard_map/correlate_tight/pallas_call | solution.py:575
  136.6 2.5 %convert_element_type.17 = f32[3,8,128,128]{3,2,1,0:T(8,128)} convert(bf16[3,8,128,128]{3,2,1,0:T(8,128)(2,1)} %get-tuple-element.39) | non-fusion elementwise | flops 393216 | bytes 2359296 | tf_op jit(solution)/shard_map/convert_element_type | solution.py:591
  (1 shorter events, 0.0 us)
